TPU v7x, 512 devices: a whole 4x4x16 slice. The times are simulated.
512 devices in a mesh: dp: 8 (over z_hi, y), expert: 64 (over z_lo, x, core).
Axes of the slice: x: 4, y: 4, z: 16 (z_hi: 2, z_lo: 8; z = z_hi * 8 + z_lo), core: 2. Of those that a mesh axis runs over, the one named last changes fastest.
Arguments:
- hidden_rows: bfloat16 [768, 65536], P(None, ('dp', 'expert')), may hold values from -6 to 6
- grad_rows: bfloat16 [65536, 2560], P(('dp', 'expert')), may hold values from -0.1796875 to 0.1796875
- block_slot: int32 [512, 1], P(('dp', 'expert')), may hold values from 0 to 1
- live_rows: int32 [512], P(('dp', 'expert')), may hold values from 16 to 128
- replica_plan: int32 [64], replicated, may hold values from 0 to 15
- master: float32 [64, 768, 640], P('expert', 'dp'), may hold values from -0.21875 to 0.21875
- moment_one: float32 [64, 768, 640], P('expert', 'dp'), may hold values from -1.8 to 1.8
- moment_two: float32 [64, 768, 640], P('expert', 'dp'), may hold values from 0.01 to 1
Outputs:
- master_new: float32 [64, 768, 640], P('expert', 'dp')
- first_new: float32 [64, 768, 640], P('expert', 'dp')
- second_new: float32 [64, 768, 640], P('expert', 'dp')
- replica_weight: bfloat16 [64, 768, 2560], P('expert', 'dp')
Inputs may be any that keep to these rules, and one draw needn't show every extreme that they name: replica_plan[j] is the expert of which the devices at index j along the expert axis host a replica; it may equal j mod 16. `block_slot`: 0 marks a block of the primary expert, 1 a block of the replica.
All inputs are finite; a program needn't handle non-finite values.
Results may differ from a plain program's by a relative error of at most 0.001.
Values may be sent and summed in bfloat16 or wider, within the bound.
A program may use at most 64 MiB of HBM per device.

v0:
```python
import jax
import jax.numpy as jnp
from jax import lax
from jax.sharding import PartitionSpec as P

QUART = 4


beta_one = 0.9
beta_two = 0.95
learn_rate = 0.01
decay_rate = 0.1
epsilon = 1e-08
step_count = 10.0


def from_behind(block, axis, distance):
    devices = range(lax.axis_size(axis))
    route = [((i - distance) % len(devices), i) for i in devices]
    return lax.ppermute(block, axis, route)


def adam_update(weights, first, second, gradient):
    first_next = beta_one * first + (1.0 - beta_one) * gradient
    second_next = beta_two * second + (1.0 - beta_two) * gradient * gradient
    scaled_first = first_next / (1.0 - beta_one**step_count)
    scaled_second = second_next / (1.0 - beta_two**step_count)
    direction = scaled_first / (jnp.sqrt(scaled_second) + epsilon)
    weights_next = weights - learn_rate * (direction + decay_rate * weights)
    return (weights_next, first_next, second_next)


def per_device(
    hidden_rows, grad_rows, block_slot, live_rows, replica_plan, master, moment_one, moment_two
):
    expert_count = lax.axis_size("expert")
    group_count = lax.axis_size("dp")
    own_index = lax.axis_index("expert")
    group_index = lax.axis_index("dp")
    hidden_units, tok_rows = hidden_rows.shape
    model_width = grad_rows.shape[1]
    block_count = block_slot.shape[1]
    block_span = tok_rows // block_count
    owner_count = expert_count // QUART
    block_width = model_width // QUART
    share_rows = hidden_units // group_count
    own_block = own_index // owner_count
    kept_rows = lax.iota(jnp.int32, tok_rows) < live_rows[0]
    row_slot = jnp.repeat(block_slot[0], block_span)
    zero_rows = jnp.zeros_like(grad_rows)
    grad_primary = jnp.where((kept_rows & (row_slot == 0))[:, None], grad_rows, zero_rows)
    grad_replica = jnp.where((kept_rows & (row_slot == 1))[:, None], grad_rows, zero_rows)
    replica_terms = jnp.dot(hidden_rows, grad_replica, preferred_element_type=jnp.float32).astype(
        jnp.bfloat16
    )
    primary_part = jnp.dot(hidden_rows, grad_primary, preferred_element_type=jnp.float32).reshape(
        hidden_units, QUART, block_width
    )
    primary_owned = lax.dynamic_index_in_dim(primary_part, own_block, 1, False)
    for step in range(1, QUART):
        target = (own_block + step) % QUART
        piece = lax.dynamic_index_in_dim(primary_part, target, 1, False)
        primary_owned = primary_owned + from_behind(piece, "expert", step * owner_count)
    expert_ids = lax.iota(jnp.int32, owner_count)
    holders = (replica_plan[None, :] == expert_ids[:, None]).astype(jnp.bfloat16)
    sectioned = replica_terms.reshape(
        expert_count, hidden_units // expert_count, QUART, block_width
    )
    pieces = lax.all_to_all(sectioned, "expert", split_axis=0, concat_axis=0, tiled=True)
    summed = jnp.einsum("es,skqd->qekd", holders, pieces, preferred_element_type=jnp.float32)
    summed = summed.reshape(expert_count, pieces.shape[1], pieces.shape[3])
    owned = lax.all_to_all(summed, "expert", split_axis=0, concat_axis=0, tiled=True).reshape(
        hidden_units, block_width
    )
    group_part = primary_owned + owned
    group_total = lax.psum(group_part, "dp")
    gradient = lax.dynamic_slice_in_dim(group_total, group_index * share_rows, share_rows, 0)
    weights_next, first_next, second_next = adam_update(
        master[0], moment_one[0], moment_two[0], gradient
    )
    fresh = weights_next.astype(jnp.bfloat16)
    chooser = (replica_plan[:, None] == expert_ids[None, :]).astype(jnp.bfloat16)
    sectioned_fresh = fresh.reshape(expert_count, 1, share_rows * block_width // expert_count)
    pieces = lax.all_to_all(sectioned_fresh, "expert", split_axis=0, concat_axis=0, tiled=True)
    grouped = pieces.reshape(QUART, owner_count, pieces.shape[1], pieces.shape[2])
    chosen = jnp.einsum(
        "je,qekc->jkqc", chooser, grouped, preferred_element_type=jnp.float32
    ).astype(jnp.bfloat16)
    received = lax.all_to_all(chosen, "expert", split_axis=0, concat_axis=0, tiled=True)
    blocks = jnp.transpose(received[:, 0], (1, 0, 2)).reshape(QUART, share_rows, block_width)
    replica_weight = jnp.transpose(blocks, (1, 0, 2)).reshape(share_rows, model_width)
    return (weights_next[None], first_next[None], second_next[None], replica_weight[None])


def solution(mesh):
    return jax.shard_map(
        per_device,
        mesh=mesh,
        in_specs=(
            P(None, ("dp", "expert")),
            P(("dp", "expert"), None),
            P(("dp", "expert"), None),
            P(("dp", "expert")),
            P(),
            P("expert", "dp", None),
            P("expert", "dp", None),
            P("expert", "dp", None),
        ),
        out_specs=(
            P("expert", "dp", None),
            P("expert", "dp", None),
            P("expert", "dp", None),
            P("expert", "dp", None),
        ),
        check_vma=False,
    )
```

profile of v0, /device:TPU:1, one launch (start us, length us, event | category | flops | bytes accessed | tf_op | source)
XLA Modules:
  0.0 983.4 jit_solution(8224352198364253314)
XLA Ops:
  7.2 0.0 copy-start
  8.5 0.0 copy-done
  8.5 4.3 fusion
  12.8 6.4 copy.50
  19.2 7.6 reshape.58
  26.8 0.0 copy-start.5
  26.8 191.5 %all_to_all.20 = bf16[64,12,4,640]{3,2,1,0:T(4,128)(2,1)S(1)} all-to-all(bf16[64,12,4,640]{3,2,1,0:T(4,128)(2,1)} %reshape.58), channel_id=1, replica_groups=mesh['dp'=8,'expert'=64] {'expert'}, dimensions={0} | all-to-all | bytes 7864320 | tf_op jit(solution)/shard_map/all_to_all | solution.py:69
  218.3 0.0 copy-done.5
  218.3 0.7 fusion.1
  219.0 2.7 copy.52
  221.7 0.0 copy-start.1
  221.7 8.7 all-to-all-start.1
  230.3 0.0 all-reduce.2.cloned.1.call-start
  230.4 0.0 copy-done.1
  230.5 1.3 fusion.8
  231.8 3.2 constant_dynamic-slice_fusion.3
  235.0 2.9 copy.47
  237.9 4.2 collective-permute-start
  242.0 2.9 copy.48
  244.9 7.2 collective-permute-start.1
  252.1 2.9 copy.49
  255.0 5.1 collective-permute-start.2
  260.1 2.9 copy.46
  262.9 276.0 %all-to-all-done.1 = f32[64,12,640]{2,1,0:T(8,128)S(1)} async-done(((f32[64,12,640]{2,1,0:T(8,128)}), f32[64,12,640]{2,1,0:T(8,128)S(1)}, u32[]{:S(2)}, u32[]{:S(2)}) %all-to-all-start.1) | async-done | bytes 1966112 | tf_op jit(solution)/shard_map/all_to_all | solution.py:72
  538.9 1.4 reshape.60
  540.4 0.0 collective-permute-done
  540.4 103.2 %collective-permute-done.1 = f32[768,640]{1,0:T(8,128)} collective-permute-done((f32[768,640]{1,0:T(8,128)}, f32[768,640]{1,0:T(8,128)}, u32[]{:S(2)}, u32[]{:S(2)}) %collective-permute-start.1) | collective-permute-done | bytes 1966112 | tf_op jit(solution)/shard_map/ppermute | solution.py:20
  643.6 0.0 collective-permute-done.2
  643.6 5.6 fusion.5
  649.2 0.0 copy-start.2
  649.2 0.0 copy-start.3
  649.2 0.0 copy-start.4
  649.2 0.0 all-reduce.2.cloned.1.call-update
  649.2 261.9 %all-reduce.2.cloned.1.call-done = f32[768,640]{1,0:T(8,128)} async-done(((f32[768,640]{1,0:T(8,128)}), f32[768,640]{1,0:T(8,128)}) %all-reduce.2.cloned.1.call-update) | async-done | bytes 1966096 | tf_op jit(solution)/shard_map/psum | solution.py:76
  911.1 0.0 copy-done.2
  911.1 0.0 copy-done.3
  911.1 0.0 copy-done.4
  911.1 1.9 fusion.27
  913.1 0.2 reshape.66
  913.3 0.5 broadcast.46
  913.8 1.4 reduce
  915.2 0.2 reshape.68
  915.4 22.3 %all_to_all.21 = bf16[64,2,480]{2,1,0:T(2,128)(2,1)S(1)} all-to-all(bf16[64,2,480]{2,1,0:T(2,128)(2,1)S(1)} %reshape.68), channel_id=1, replica_groups=mesh['dp'=8,'expert'=64] {'expert'}, dimensions={0} | all-to-all | bytes 245760 | tf_op jit(solution)/shard_map/all_to_all | solution.py:84
  937.6 0.2 reshape.69
  937.9 0.3 fusion.6
  938.2 0.4 copy.54
  938.6 35.7 %all_to_all.22 = bf16[64,1,4,960]{3,2,1,0:T(4,128)(2,1)S(1)} all-to-all(bf16[64,1,4,960]{3,2,1,0:T(4,128)(2,1)S(1)} %copy.54), channel_id=1, replica_groups=mesh['dp'=8,'expert'=64] {'expert'}, dimensions={0} | all-to-all | bytes 983040 | tf_op jit(solution)/shard_map/all_to_all | solution.py:89
  974.3 0.2 copy.55
  974.5 0.8 reshape.63
  975.3 0.3 copy.56
  975.5 1.0 broadcast_in_dim_reshape.3
  (2 shorter events, 0.1 us)
Async XLA Ops:
  7.2 1.4 copy-start
  26.8 191.5 %copy-start.5 = (s32[64]{0:T(128)S(1)}, s32[64]{0:T(128)}, u32[]{:S(2)}) copy-start(s32[64]{0:T(128)} %param.12) | copy-start | bytes 772
  221.7 8.8 copy-start.1
  221.7 317.3 %all-to-all-start.1 = ((f32[64,12,640]{2,1,0:T(8,128)}), f32[64,12,640]{2,1,0:T(8,128)S(1)}, u32[]{:S(2)}, u32[]{:S(2)}) async-start(f32[64,12,640]{2,1,0:T(8,128)} %copy.52), calls=%async_computation.1 | async-start | bytes 5242880 | tf_op jit(solution)/shard_map/all_to_all | solution.py:72
  230.3 680.8 %all-reduce.2.cloned.1.call-start = ((), (), s32[]{:S(2)}) async-start(), calls=%async_computation.4 | async-start | bytes 3932160 | tf_op jit(solution)/shard_map/psum | solution.py:76
  237.9 302.5 %collective-permute-start = (f32[768,640]{1,0:T(8,128)}, f32[768,640]{1,0:T(8,128)}, u32[]{:S(2)}, u32[]{:S(2)}) collective-permute-start(f32[768,640]{1,0:T(8,128)} %bitcast.75), channel_id=1, source_target_pairs={{48,0},{49,1},{50,2},{51,3},{52,4},{53,5},{54,6},{55,7},{56,8},{57... | collective-permute-start | bytes 5898248 | tf_op jit(solution)/shard_map/ppermute | solution.py:20
  244.9 398.7 %collective-permute-start.1 = (f32[768,640]{1,0:T(8,128)}, f32[768,640]{1,0:T(8,128)}, u32[]{:S(2)}, u32[]{:S(2)}) collective-permute-start(f32[768,640]{1,0:T(8,128)} %bitcast.76), channel_id=1, source_target_pairs={{32,0},{33,1},{34,2},{35,3},{36,4},{37,5},{38,6},{39,7},{40,8},{41... | collective-permute-start | bytes 5898248 | tf_op jit(solution)/shard_map/ppermute | solution.py:20
  255.0 388.6 %collective-permute-start.2 = (f32[768,640]{1,0:T(8,128)}, f32[768,640]{1,0:T(8,128)}, u32[]{:S(2)}, u32[]{:S(2)}) collective-permute-start(f32[768,640]{1,0:T(8,128)} %bitcast.77), channel_id=1, source_target_pairs={{16,0},{17,1},{18,2},{19,3},{20,4},{21,5},{22,6},{23,7},{24,8},{25... | collective-permute-start | bytes 5898248 | tf_op jit(solution)/shard_map/ppermute | solution.py:20
  649.2 261.9 %copy-start.2 = (f32[1,96,640]{2,1,0:T(8,128)S(1)}, f32[1,96,640]{2,1,0:T(8,128)}, u32[]{:S(2)}) copy-start(f32[1,96,640]{2,1,0:T(8,128)} %param.15) | copy-start | bytes 737284
  649.2 261.9 %copy-start.3 = (f32[1,96,640]{2,1,0:T(8,128)S(1)}, f32[1,96,640]{2,1,0:T(8,128)}, u32[]{:S(2)}) copy-start(f32[1,96,640]{2,1,0:T(8,128)} %param.14) | copy-start | bytes 737284
  649.2 261.9 %copy-start.4 = (f32[1,96,640]{2,1,0:T(8,128)S(1)}, f32[1,96,640]{2,1,0:T(8,128)}, u32[]{:S(2)}) copy-start(f32[1,96,640]{2,1,0:T(8,128)} %param.13) | copy-start | bytes 737284
Sparse Core Ops, SparseCore 0:
  649.3 261.7 all-reduce.1
where the time goes:
time: 988 us; the launch traced here: 983 us
  waiting for transfers between devices  641 us (65%)
  blocking collectives  249 us (25%)
  local copies, waits for them, and re-layouts  36.5 us (4%)
  starting transfers between devices  25.1 us (3%)
  between operations  15.6 us (2%)
    all_to_all x1, waiting for transfers between devices, per_device(): lax.all_to_all(summed, 'expert', split_axis=0, concat_axis=0, tiled=True)  276 us
    psum x1, waiting for transfers between devices, per_device(): group_total = lax.psum(group_part, 'dp')  262 us
    all_to_all x1, blocking collectives, per_device(): lax.all_to_all(sectioned, 'expert', split_axis=0, concat_axis=0, tiled=True)  191 us
    ppermute x3, waiting for transfers between devices, from_behind(): return lax.ppermute(block, axis, route)  103 us
    all_to_all x1, blocking collectives, per_device(): lax.all_to_all(chosen, 'expert', split_axis=0, concat_axis=0, tiled=True)  35.7 us
    all_to_all x1, blocking collectives, per_device(): lax.all_to_all(sectioned_fresh, 'expert', split_axis=0, concat_axis=0, ti...  22.3 us
  transfers between devices with their start and end apart: 5, of which 3 were waited for; matrix products, arithmetic and copies ran while one was open for 2% of the time, Pallas kernels for 0%

commit v1 on v0

v1 whole, which is shorter than its diff:
```python
import functools

import jax
import jax.numpy as jnp
from jax import lax
from jax.experimental import pallas as pl
from jax.experimental.pallas import tpu as pltpu
from jax.sharding import PartitionSpec as P

MESH = pl.DeviceIdType.MESH

N_Y, N_X, N_C, N_LO, N_HI = 4, 4, 2, 8, 2
N_Z = N_HI * N_LO
N_HOST = N_X * N_C
QUART = 4
EXPERTS = 16
FLAG_ROWS = 16
SUBS = 3

beta_one = 0.9
beta_two = 0.95
learn_rate = 0.01
decay_rate = 0.1
epsilon = 1e-08
step_count = 10.0


def adam_update(weights, first, second, gradient):
    first_next = beta_one * first + (1.0 - beta_one) * gradient
    second_next = beta_two * second + (1.0 - beta_two) * gradient * gradient
    scaled_first = first_next / (1.0 - beta_one**step_count)
    scaled_second = second_next / (1.0 - beta_two**step_count)
    direction = scaled_first / (jnp.sqrt(scaled_second) + epsilon)
    weights_next = weights - learn_rate * (direction + decay_rate * weights)
    return (weights_next, first_next, second_next)


def place():
    g = lax.axis_index("dp")
    j = lax.axis_index("expert")
    z_hi, y = lax.div(g, N_Y), lax.rem(g, N_Y)
    z_lo, x, c = lax.div(j, N_HOST), lax.rem(lax.div(j, N_C), N_X), lax.rem(j, N_C)
    return z_hi, z_lo, y, x, c


def device(z_hi, z_lo, y, x, c):
    return (z_hi * N_Y + y, z_lo * N_HOST + x * N_C + c)


def wrap(v, n):
    return lax.rem(v + n, n)


def slot_at(p, x, c):
    return lax.rem(5 * p + 6 + 4 * x + 8 * c, EXPERTS)


def position_of(e, x, c):
    return lax.rem(13 * (e + 42 - 4 * x - 8 * c), N_Z)


def gradient_kernel(
    plan_ref, hid_ref, grad_ref, out_ref,
    hall, gall, prim, repl, term, ring,
    own_sem, hs1, hr1, hs2, hr2, gs_x, gs_y, gs_h, gs_c, gr, rs, rr, fs, fr,
):
    z_hi, z_lo, y, x, c = place()
    z = z_hi * N_LO + z_lo
    rows, width = out_ref.shape
    half = rows // 2
    sub = half // SUBS
    tok = grad_ref.shape[0]
    up, down = wrap(z + 1, N_Z), wrap(z - 1, N_Z)
    dev_up = device(lax.div(up, N_LO), lax.rem(up, N_LO), y, x, c)
    dev_down = device(lax.div(down, N_LO), lax.rem(down, N_LO), y, x, c)
    e_mine = slot_at(z, x, c)
    dev_to = device(
        c, 2 * x + lax.div(e_mine, N_HOST), y,
        lax.rem(lax.div(e_mine, N_C), N_X), lax.rem(e_mine, N_C),
    )
    e_own = lax.rem(z_lo, 2) * N_HOST + x * N_C + c
    x_from = lax.div(z_lo, 2)
    z_from = position_of(e_own, x_from, z_hi)
    dev_from = device(lax.div(z_from, N_LO), lax.rem(z_from, N_LO), y, x_from, z_hi)

    def here(yy, xx, cc):
        return device(z_hi, z_lo, yy, xx, cc)

    y_next, y_prev = wrap(y + 1, N_Y), wrap(y - 1, N_Y)
    partner = here(y, x, 1 - c)
    yc_peers = [
        (wrap(y + dy, N_Y), c if dc == 0 else 1 - c)
        for dy in range(N_Y) for dc in range(N_C) if (dy, dc) != (0, 0)
    ]
    x_peers = [wrap(x + dx, N_X) for dx in range(1, N_X)]
    me8 = y * N_C + c

    def source(yy, xx, cc):
        return (yy * N_X + xx) * N_C + cc

    own_cols = pl.ds(pl.multiple_of(x * width, 128), width)
    own_g = pltpu.make_async_copy(grad_ref.at[:, own_cols], gall.at[source(y, x, c)], own_sem.at[0])
    own_h = pltpu.make_async_copy(hid_ref.at[c * N_Y + y], hall.at[x, me8], own_sem.at[1])
    own_g.start()
    own_h.start()

    barrier = pltpu.get_barrier_semaphore()
    greeted = [here(yy, x, cc) for yy, cc in yc_peers] + [here(y, xx, c) for xx in x_peers]
    greeted += [dev_up, dev_down, dev_to, dev_from]
    for dev in greeted:
        pl.semaphore_signal(barrier, inc=1, device_id=dev, device_id_type=MESH)
    pl.semaphore_wait(barrier, len(greeted))

    def remote(src, dst, ssem, rsem, dev):
        return pltpu.make_async_remote_copy(
            src_ref=src, dst_ref=dst, send_sem=ssem, recv_sem=rsem,
            device_id=dev, device_id_type=MESH,
        )

    h1 = []
    for k, (yy, cc) in enumerate(yc_peers):
        h1.append(remote(hid_ref.at[cc * N_Y + yy], hall.at[x, me8], hs1.at[k], hr1.at[k], here(yy, x, cc)))
        h1[-1].start()
    gx = []
    for k, xx in enumerate(x_peers):
        cols = pl.ds(pl.multiple_of(xx * width, 128), width)
        s = source(y, x, c)
        gx.append(remote(grad_ref.at[:, cols], gall.at[s], gs_x.at[k], gr.at[k + 1, 0], here(y, xx, c)))
        gx[-1].start()

    prim[...] = jnp.zeros_like(prim)
    repl[...] = jnp.zeros_like(repl)

    own_h.wait()
    for copy in h1:
        copy.wait_recv()
    h2 = []
    for k, xx in enumerate(x_peers):
        h2.append(remote(hall.at[x], hall.at[x], hs2.at[k], hr2.at[k], here(y, xx, c)))
        h2[-1].start()

    def add_product(yy, xx, cc):
        block = hall.at[xx, yy * N_C + cc]
        product = jnp.dot(
            block[pl.ds(0, rows), :], gall[source(yy, xx, cc)], preferred_element_type=jnp.float32
        )
        flag = block[pl.ds(rows, FLAG_ROWS), :].astype(jnp.float32)[0:1, :]
        flag = jnp.concatenate([jnp.broadcast_to(flag, (rows, 128))] * (width // 128), axis=1)
        host = xx * N_C + cc
        rounded = product.astype(jnp.bfloat16).astype(jnp.float32)
        prim[host] += jnp.where(flag > 0.5, 0.0, product)
        repl[host] += jnp.where(flag > 0.5, rounded, 0.0)

    top, bottom = pl.ds(0, tok // 2), pl.ds(tok // 2, tok // 2)

    def to_partner(group, dx, s):
        return remote(gall.at[s], gall.at[s], gs_c.at[group, dx], gr.at[(4 + group) * 4 + dx, 0], partner)

    def full(s, group, dx, dev):
        return remote(gall.at[s], gall.at[s], gs_y.at[0, dx], gr.at[group * 4 + dx, 0], dev)

    def group_own(dx, carry):
        xx = wrap(x - dx, N_X)
        s = source(y, xx, c)

        @pl.when(dx == 0)
        def _():
            own_g.wait()

        @pl.when(dx > 0)
        def _():
            full(s, 0, dx, partner).wait_recv()

        remote(gall.at[s], gall.at[s], gs_y.at[0, dx], gr.at[4 + dx, 0], here(y_next, x, c)).start()
        remote(gall.at[s], gall.at[s], gs_y.at[1, dx], gr.at[8 + dx, 0], here(y_prev, x, c)).start()
        to_partner(0, dx, s).start()

        @pl.when(dx == 0)
        def _():
            for copy in h2:
                copy.wait_recv()

        add_product(y, xx, c)
        return carry

    lax.fori_loop(0, N_X, group_own, 0)

    def group_prev(dx, carry):
        xx = wrap(x - dx, N_X)
        s = source(y_prev, xx, c)
        full(s, 1, dx, partner).wait_recv()
        remote(
            gall.at[s, top], gall.at[s, top], gs_h.at[0, dx], gr.at[12 + dx, 0], here(y_next, x, c)
        ).start()
        to_partner(1, dx, s).start()
        s2 = source(y_next, xx, c)
        full(s2, 2, dx, partner).wait_recv()
        remote(
            gall.at[s2, bottom], gall.at[s2, bottom], gs_h.at[1, dx], gr.at[12 + dx, 1], here(y_prev, x, c)
        ).start()
        to_partner(2, dx, s2).start()
        add_product(y_prev, xx, c)
        add_product(y_next, xx, c)
        return carry

    lax.fori_loop(0, N_X, group_prev, 0)

    y_far = wrap(y + 2, N_Y)

    def group_far(dx, carry):
        xx = wrap(x - dx, N_X)
        s = source(y_far, xx, c)
        remote(
            gall.at[s, top], gall.at[s, top], gs_h.at[0, dx], gr.at[12 + dx, 0], partner
        ).wait_recv()
        remote(
            gall.at[s, bottom], gall.at[s, bottom], gs_h.at[1, dx], gr.at[12 + dx, 1], partner
        ).wait_recv()
        to_partner(3, dx, s).start()
        add_product(y_far, xx, c)
        return carry

    lax.fori_loop(0, N_X, group_far, 0)

    def group_partner(k, carry):
        group, dx = lax.div(k, N_X), lax.rem(k, N_X)
        yy = wrap(y + jnp.where(group == 1, N_Y - 1, jnp.where(group == 2, 1, jnp.where(group == 3, 2, 0))), N_Y)
        xx = wrap(x - dx, N_X)
        s = source(yy, xx, 1 - c)
        remote(
            gall.at[s], gall.at[s], gs_c.at[group, dx], gr.at[(4 + group) * 4 + dx, 0], partner
        ).wait_recv()
        add_product(yy, xx, 1 - c)
        return carry

    lax.fori_loop(0, 4 * N_X, group_partner, 0)

    parity = lax.rem(z_lo, 2)

    def make_term(s):
        for d in range(2):
            p = wrap(z - 1 - s, N_Z) if d == 0 else wrap(z + 1 + s, N_Z)
            p = lax.rem(p + N_Z, N_Z)
            e = slot_at(p, x, c)
            span = pl.ds(d * half, half)
            weight = jnp.where(lax.div(e, N_HOST) == parity, 1.0, 0.0)
            total = prim[lax.rem(e, N_HOST), span, :] * weight
            for h in range(N_HOST):
                weight = jnp.where(plan_ref[z_lo * N_HOST + h] == e, 1.0, 0.0)
                total += repl[h, span, :] * weight
            term[d, s] = total

    def ring_copy(d, s, u, src):
        return remote(
            src, ring.at[d, s, pl.ds(u * sub, sub)], rs.at[d, s, u], rr.at[d, s, u],
            dev_up if d == 0 else dev_down,
        )

    make_term(0)
    for u in range(SUBS):
        for d in range(2):
            ring_copy(d, 0, u, term.at[d, 0, pl.ds(u * sub, sub)]).start()
    make_term(1)

    def ring_step(s, carry):
        for u in range(SUBS):
            for d in range(2):
                part = pl.ds(u * sub, sub)
                ring_copy(d, s - 1, u, ring.at[d, s - 1, part]).wait_recv()
                ring[d, s - 1, part, :] += term[d, s, part, :]
                ring_copy(d, s, u, ring.at[d, s - 1, part]).start()
        make_term(s + 1)
        return carry

    lax.fori_loop(1, N_Z - 1, ring_step, 0)

    last = []
    for u in range(SUBS):
        for d in range(2):
            part = pl.ds(u * sub, sub)
            ring_copy(d, N_Z - 2, u, ring.at[d, N_Z - 2, part]).wait_recv()
            ring[d, N_Z - 2, part, :] += term[d, N_Z - 1, part, :]
            copy = remote(
                ring.at[d, N_Z - 2, part], out_ref.at[pl.ds(d * half + u * sub, sub)],
                fs.at[d, u], fr.at[d, u], dev_to,
            )
            copy.start()
            last.append(copy)

    for copy in h1 + h2 + gx:
        copy.wait_send()

    def drain(dx, carry):
        whole = gall.at[source(y, x, c)]
        part = gall.at[source(y, x, c), top]
        for k in range(2):
            remote(whole, whole, gs_y.at[k, dx], gr.at[0, 0], partner).wait_send()
            remote(part, part, gs_h.at[k, dx], gr.at[0, 0], partner).wait_send()
        for k in range(4):
            remote(whole, whole, gs_c.at[k, dx], gr.at[0, 0], partner).wait_send()
        return carry

    lax.fori_loop(0, N_X, drain, 0)

    def drain_ring(s, carry):
        for u in range(SUBS):
            for d in range(2):
                ring_copy(d, s, u, term.at[d, 0, pl.ds(u * sub, sub)]).wait_send()
        return carry

    lax.fori_loop(0, N_Z - 1, drain_ring, 0)
    for copy in last:
        copy.wait()


def weights_kernel(plan_ref, fresh_ref, out_ref, line, mixed, picked, own_sem, ls, lr, ms, mr, ps, pr):
    z_hi, z_lo, y, x, c = place()
    rows, width = fresh_ref.shape
    half = rows // 2

    def here(zz, xx, cc):
        return device(z_hi, zz, y, xx, cc)

    right, left = wrap(z_lo + 1, N_LO), wrap(z_lo - 1, N_LO)
    plane = [(dx, dc) for dx in range(N_X) for dc in range(N_C)]

    def peer(dx, dc):
        return wrap(x + dx, N_X), (c if dc == 0 else 1 - c)

    own = pltpu.make_async_copy(fresh_ref, line.at[z_lo], own_sem.at[0])
    own.start()
    barrier = pltpu.get_barrier_semaphore()
    greeted = [here(z_lo, *peer(dx, dc)) for dx, dc in plane[1:]]
    greeted += [here(right, x, c), here(left, x, c)]
    for dev in greeted:
        pl.semaphore_signal(barrier, inc=1, device_id=dev, device_id_type=MESH)
    pl.semaphore_wait(barrier, len(greeted))
    own.wait()

    def remote(src, dst, ssem, rsem, dev):
        return pltpu.make_async_remote_copy(
            src_ref=src, dst_ref=dst, send_sem=ssem, recv_sem=rsem,
            device_id=dev, device_id_type=MESH,
        )

    def line_copy(d, k):
        return remote(line.at[k], line.at[k], ls.at[d, k], lr.at[k], here(right if d == 0 else left, x, c))

    def mix_copy(k, cc):
        q, b = lax.div(k, 2), lax.rem(k, 2)
        e = b * N_HOST + x * N_C + c
        dist = wrap(q - x, N_X)
        apart = jnp.where(cc == c, 0, 1)
        src = line.at[k, pl.ds(cc * half, half)]
        return remote(
            src, mixed.at[e], ms.at[k, cc], mr.at[b, dist, apart], here(z_lo, q, cc)
        )

    def local_mix(k):
        b = lax.rem(k, 2)
        return pltpu.make_async_copy(
            line.at[k, pl.ds(pl.multiple_of(c * half, 16), half)],
            mixed.at[b * N_HOST + x * N_C + c], own_sem.at[1 + b],
        )

    def scatter(k):
        q = lax.div(k, 2)
        for cc in range(N_C):
            mine = (q == x) & (cc == c)

            @pl.when(mine)
            def _():
                local_mix(k).start()

            @pl.when(jnp.logical_not(mine))
            def _():
                mix_copy(k, cc).start()

    @pl.when(z_lo < N_LO - 1)
    def _():
        line_copy(0, z_lo).start()

    @pl.when(z_lo > 0)
    def _():
        line_copy(1, z_lo).start()

    scatter(z_lo)

    def line_step(t, carry):
        k = z_lo - t

        @pl.when(k >= 0)
        def _():
            line_copy(0, k).wait_recv()

            @pl.when(z_lo < N_LO - 1)
            def _():
                line_copy(0, k).start()

            scatter(k)

        k2 = z_lo + t

        @pl.when(k2 < N_LO)
        def _():
            line_copy(1, k2).wait_recv()

            @pl.when(z_lo > 0)
            def _():
                line_copy(1, k2).start()

            scatter(k2)

        return carry

    lax.fori_loop(1, N_LO, line_step, 0)

    for b in range(2):
        local_mix(2 * x + b).wait()
        for dx, dc in plane[1:]:
            piece = mixed.at[0]
            remote(piece, piece, ms.at[0, 0], mr.at[b, dx, dc], here(z_lo, *peer(1, 0))).wait_recv()

    mine = out_ref.at[pl.ds(pl.multiple_of(c * half, 16), half), pl.ds(pl.multiple_of(x * width, 128), width)]
    sends = []
    for n, (dx, dc) in enumerate(plane):
        xx, cc = peer(dx, dc)
        picked[n] = mixed[plan_ref[z_lo * N_HOST + xx * N_C + cc]]
        if n == 0:
            sends.append(pltpu.make_async_copy(picked.at[0], mine, own_sem.at[3]))
        else:
            sends.append(remote(picked.at[n], mine, ps.at[n], pr.at[n], here(z_lo, xx, cc)))
        sends[-1].start()

    def drain(k, carry):
        @pl.when((z_lo < N_LO - 1) & (k <= z_lo))
        def _():
            line_copy(0, k).wait_send()

        @pl.when((z_lo > 0) & (k >= z_lo))
        def _():
            line_copy(1, k).wait_send()

        for cc in range(N_C):
            @pl.when(jnp.logical_not((lax.div(k, 2) == x) & (cc == c)))
            def _():
                mix_copy(k, cc).wait_send()

        return carry

    lax.fori_loop(0, N_LO, drain, 0)
    for copy in sends:
        copy.wait()


def per_device(
    hidden_rows, grad_rows, block_slot, live_rows, replica_plan, master, moment_one, moment_two
):
    hidden_units, tok = hidden_rows.shape
    model_width = grad_rows.shape[1]
    groups = N_HI * N_Y
    rows = hidden_units // groups
    width = model_width // QUART
    half = rows // 2
    kept = lax.iota(jnp.int32, tok) < live_rows[0]
    masked = jnp.where(kept[None, :], hidden_rows, jnp.zeros_like(hidden_rows)).reshape(groups, rows, tok)
    flags = jnp.broadcast_to((block_slot[0, 0] == 1).astype(jnp.bfloat16), (groups, FLAG_ROWS, tok))
    hid = jnp.concatenate([masked, flags], axis=1)
    sub = half // SUBS
    dma = pltpu.SemaphoreType.DMA
    gradient = pl.pallas_call(
        gradient_kernel,
        out_shape=jax.ShapeDtypeStruct((rows, width), jnp.float32),
        in_specs=[
            pl.BlockSpec(memory_space=pltpu.SMEM),
            pl.BlockSpec(memory_space=pl.ANY),
            pl.BlockSpec(memory_space=pl.ANY),
        ],
        out_specs=pl.BlockSpec(memory_space=pltpu.VMEM),
        scratch_shapes=[
            pltpu.VMEM((N_X, N_Y * N_C, rows + FLAG_ROWS, tok), jnp.bfloat16),
            pltpu.VMEM((N_Y * N_X * N_C, tok, width), jnp.bfloat16),
            pltpu.VMEM((N_HOST, rows, width), jnp.float32),
            pltpu.VMEM((N_HOST, rows, width), jnp.float32),
            pltpu.VMEM((2, N_Z, half, width), jnp.float32),
            pltpu.VMEM((2, N_Z - 1, half, width), jnp.float32),
            dma((2,)), dma((7,)), dma((7,)), dma((3,)), dma((3,)),
            dma((3,)), dma((2, 4)), dma((2, 4)), dma((4, 4)), dma((32, 2)),
            dma((2, N_Z - 1, SUBS)), dma((2, N_Z - 1, SUBS)), dma((2, SUBS)), dma((2, SUBS)),
        ],
        compiler_params=pltpu.CompilerParams(
            collective_id=0, has_side_effects=True, vmem_limit_bytes=40 * 2**20
        ),
        name="gradient",
    )(replica_plan, hid, grad_rows)
    weights_next, first_next, second_next = adam_update(
        master[0], moment_one[0], moment_two[0], gradient
    )
    fresh = weights_next.astype(jnp.bfloat16)
    replica_weight = pl.pallas_call(
        weights_kernel,
        out_shape=jax.ShapeDtypeStruct((rows, model_width), jnp.bfloat16),
        in_specs=[
            pl.BlockSpec(memory_space=pltpu.SMEM),
            pl.BlockSpec(memory_space=pltpu.VMEM),
        ],
        out_specs=pl.BlockSpec(memory_space=pltpu.VMEM),
        scratch_shapes=[
            pltpu.VMEM((N_LO, rows, width), jnp.bfloat16),
            pltpu.VMEM((EXPERTS, half, width), jnp.bfloat16),
            pltpu.VMEM((N_HOST, half, width), jnp.bfloat16),
            dma((4,)), dma((2, N_LO)), dma((N_LO,)), dma((N_LO, N_C)), dma((2, N_X, N_C)),
            dma((N_HOST,)), dma((N_HOST,)),
        ],
        compiler_params=pltpu.CompilerParams(
            collective_id=1, has_side_effects=True, vmem_limit_bytes=16 * 2**20
        ),
        name="weights",
    )(replica_plan, fresh)
    return (weights_next[None], first_next[None], second_next[None], replica_weight[None])


def solution(mesh):
    return jax.shard_map(
        per_device,
        mesh=mesh,
        in_specs=(
            P(None, ("dp", "expert")),
            P(("dp", "expert"), None),
            P(("dp", "expert"), None),
            P(("dp", "expert")),
            P(),
            P("expert", "dp", None),
            P("expert", "dp", None),
            P("expert", "dp", None),
        ),
        out_specs=(
            P("expert", "dp", None),
            P("expert", "dp", None),
            P("expert", "dp", None),
            P("expert", "dp", None),
        ),
        check_vma=False,
    )
```

time: 988 us -> 198 us (0.20)
  waiting for transfers between devices: 641 us -> 0 us
  blocking collectives: 249 us -> 0 us
  Pallas kernels: 0 us -> 192 us
  local copies, waits for them, and re-layouts: 36.5 us -> 1.43 us
  starting transfers between devices: 25.1 us -> 0 us
  between operations: 15.6 us -> 2.08 us
    all_to_all x1 -> x0, waiting for transfers between devices: 276 us -> none  [per_device(): lax.all_to_all(summed, 'expert', split_axis=0, concat_axis=0, tiled=True)]
    psum x1 -> x0, waiting for transfers between devices: 262 us -> none  [per_device(): group_total = lax.psum(group_part, 'dp')]
    all_to_all x3 -> x0, blocking collectives: 249 us -> none  [the longest x1 191 us: per_device(): lax.all_to_all(sectioned, 'expert', split_axis=0, concat_axis=0, tiled=True)]
    pallas_call x0 -> x2, Pallas kernels: none -> 192 us  [the longest x1 127 us: per_device(): pl.pallas_call(gradient_kernel, out_shape=jax.ShapeDtypeStruct((rows, wid...]
    ppermute x3 -> x0, waiting for transfers between devices: 103 us -> none  [from_behind(): return lax.ppermute(block, axis, route)]
    ppermute x3 -> x0, starting transfers between devices: 16.4 us -> none  [from_behind(): return lax.ppermute(block, axis, route)]
    dynamic_slice x5 -> x0, local copies, waits for them, and re-layouts: 14.7 us -> none  [the longest x3 8.63 us: per_device(): piece = lax.dynamic_index_in_dim(primary_part, target, 1, False)]
    reshape x6 -> x0, local copies, waits for them, and re-layouts: 13.2 us -> none  [the longest x1 7.61 us: per_device(): replica_terms.reshape(expert_count, hidden_units // expert_count, QUART,...]
  transfers between devices with their start and end apart: 5 -> 0, of which waited for: 3 -> 0; matrix products, arithmetic and copies ran while one was open for 2% -> 0% of each run, Pallas kernels for 0% -> 0%
where the time goes in v1:
time: 198 us; the launch traced here: 197 us
  Pallas kernels  192 us (97%)
  between operations  2.08 us (1%)
    pallas_call x1, Pallas kernels, per_device(): pl.pallas_call(gradient_kernel, out_shape=jax.ShapeDtypeStruct((rows, wid...  127 us
    pallas_call x1, Pallas kernels, per_device(): pl.pallas_call(weights_kernel, out_shape=jax.ShapeDtypeStruct((rows, mode...  65.1 us

profile of v1, /device:TPU:1, one launch (start us, length us, event | category | flops | bytes accessed | tf_op | source)
XLA Modules:
  0.0 197.3 jit_solution(15339121043304681289)
XLA Ops:
  0.6 0.0 copy-start
  2.0 0.9 broadcast_select_fusion
  3.0 0.0 copy-start.1
  3.0 0.0 copy-done
  3.0 0.6 copy-done.1
  3.6 0.0 copy-start.2
  3.6 0.0 copy-start.3
  3.6 0.0 copy-start.4
  3.6 126.7 %gradient.1 = f32[96,640]{1,0:T(8,128)S(1)} custom-call(s32[64]{0:T(128)S(1)} %copy-done.1, bf16[8,112,128]{2,1,0:T(8,128)(2,1)S(1)} %concatenate.3.hid_ref, bf16[128,2560]{1,0:T(8,128)(2,1)S(1)} %copy-done), custom_call_target="tpu_custom_call" | custom-call | tf_op jit(solution)/shard_map/gradient/pallas_call | solution.py:471
  130.4 0.0 copy-done.2
  130.4 0.0 copy-done.3
  130.4 0.0 copy-done.4
  130.4 1.0 fusion.5
  131.4 65.1 %weights.1 = bf16[96,2560]{1,0:T(8,128)(2,1)S(1)} custom-call(s32[64]{0:T(128)S(1)} %copy-done.1, bf16[96,640]{1,0:T(8,128)(2,1)S(1)} %get-tuple-element.4.fresh_ref), custom_call_target="tpu_custom_call" | custom-call | tf_op jit(solution)/shard_map/weights/pallas_call | solution.py:500
  196.5 0.8 copy.15
  (2 shorter events, 0.0 us)
Async XLA Ops:
  0.6 2.4 %copy-start = (bf16[128,2560]{1,0:T(8,128)(2,1)S(1)}, bf16[128,2560]{1,0:T(8,128)(2,1)}, u32[]{:S(2)}) copy-start(bf16[128,2560]{1,0:T(8,128)(2,1)} %grad_ref.1) | copy-start | bytes 1966084
  3.0 0.7 copy-start.1
  3.6 126.8 %copy-start.2 = (f32[1,96,640]{2,1,0:T(8,128)S(1)}, f32[1,96,640]{2,1,0:T(8,128)}, u32[]{:S(2)}) copy-start(f32[1,96,640]{2,1,0:T(8,128)} %param.15) | copy-start | bytes 737284
  3.6 126.8 %copy-start.3 = (f32[1,96,640]{2,1,0:T(8,128)S(1)}, f32[1,96,640]{2,1,0:T(8,128)}, u32[]{:S(2)}) copy-start(f32[1,96,640]{2,1,0:T(8,128)} %param.14) | copy-start | bytes 737284
  3.6 126.8 %copy-start.4 = (f32[1,96,640]{2,1,0:T(8,128)S(1)}, f32[1,96,640]{2,1,0:T(8,128)}, u32[]{:S(2)}) copy-start(f32[1,96,640]{2,1,0:T(8,128)} %param.13) | copy-start | bytes 737284

commit v2 on v0

v2 whole, which is shorter than its diff:
```python
import functools

import jax
import jax.numpy as jnp
from jax import lax
from jax.experimental import pallas as pl
from jax.experimental.pallas import tpu as pltpu
from jax.sharding import PartitionSpec as P

MESH = pl.DeviceIdType.MESH

N_Y, N_X, N_C, N_LO, N_HI = 4, 4, 2, 8, 2
N_Z = N_HI * N_LO
N_HOST = N_X * N_C
QUART = 4
EXPERTS = 16
FLAG_ROWS = 16
CHUNKS = ((0, 384), (384, 256))

beta_one = 0.9
beta_two = 0.95
learn_rate = 0.01
decay_rate = 0.1
epsilon = 1e-08
step_count = 10.0


def adam_update(weights, first, second, gradient):
    first_next = beta_one * first + (1.0 - beta_one) * gradient
    second_next = beta_two * second + (1.0 - beta_two) * gradient * gradient
    scaled_first = first_next / (1.0 - beta_one**step_count)
    scaled_second = second_next / (1.0 - beta_two**step_count)
    direction = scaled_first / (jnp.sqrt(scaled_second) + epsilon)
    weights_next = weights - learn_rate * (direction + decay_rate * weights)
    return (weights_next, first_next, second_next)


def place():
    g = lax.axis_index("dp")
    j = lax.axis_index("expert")
    z_hi, y = lax.div(g, N_Y), lax.rem(g, N_Y)
    z_lo, x, c = lax.div(j, N_HOST), lax.rem(lax.div(j, N_C), N_X), lax.rem(j, N_C)
    return z_hi, z_lo, y, x, c


def device(z_hi, z_lo, y, x, c):
    return (z_hi * N_Y + y, z_lo * N_HOST + x * N_C + c)


def wrap(v, n):
    return lax.rem(v + n, n)


def gradient_kernel(
    plan_ref, hid_ref, grad_ref, out_ref,
    hall, gall, prim, repl, ring,
    own_sem, hs1, hr1, hs2, hr2, gxs, gr, gys, gyh, gcs, gcr, rs, rr, fs, fr,
):
    z_hi, z_lo, y, x, c = place()
    z = z_hi * N_LO + z_lo
    rows, width = out_ref.shape
    half = rows // 2
    tok = grad_ref.shape[0]

    def here(yy, xx, cc):
        return device(z_hi, z_lo, yy, xx, cc)

    def level(zz):
        return device(lax.div(zz, N_LO), lax.rem(zz, N_LO), y, x, c)

    y_next, y_prev, y_far = wrap(y + 1, N_Y), wrap(y - 1, N_Y), wrap(y + 2, N_Y)
    partner = here(y, x, 1 - c)
    yc_peers = [
        (wrap(y + dy, N_Y), c if dc == 0 else 1 - c)
        for dy in range(N_Y) for dc in range(N_C) if (dy, dc) != (0, 0)
    ]
    x_peers = [wrap(x + dx, N_X) for dx in range(1, N_X)]
    xc_peers = [(xx, cc) for xx in x_peers for cc in (c, 1 - c)]
    me8 = y * N_C + c

    def source(yy, xx, cc):
        return (yy * N_X + xx) * N_C + cc

    me = source(y, x, c)

    def columns(q, ch):
        return pl.ds(pl.multiple_of(q * width + CHUNKS[ch][0], 128), CHUNKS[ch][1])

    def span(ch):
        return pl.ds(*CHUNKS[ch])

    own_cols = pl.ds(pl.multiple_of(x * width, 128), width)
    own_g = pltpu.make_async_copy(grad_ref.at[:, own_cols], gall.at[me], own_sem.at[0])
    own_h = pltpu.make_async_copy(hid_ref.at[c * N_Y + y], hall.at[x, me8], own_sem.at[1])
    own_h.start()
    own_g.start()

    barrier = pltpu.get_barrier_semaphore()
    greeted = [here(yy, x, cc) for yy, cc in yc_peers] + [here(y, xx, cc) for xx, cc in xc_peers]
    greeted += [level(wrap(z + 1, N_Z)), level(wrap(z - 1, N_Z))]
    for dev in greeted:
        pl.semaphore_signal(barrier, inc=1, device_id=dev, device_id_type=MESH)
    pl.semaphore_wait(barrier, len(greeted))

    def remote(src, dst, ssem, rsem, dev):
        return pltpu.make_async_remote_copy(
            src_ref=src, dst_ref=dst, send_sem=ssem, recv_sem=rsem,
            device_id=dev, device_id_type=MESH,
        )

    def loop(first, count, body):
        def one(k, carry):
            body(k)
            return carry

        lax.fori_loop(first, first + count, one, 0)

    parts = (pl.ds(0, tok // 2), pl.ds(tok // 2, tok // 2))
    rows_of = (y, y_prev, y_next, y_far)

    def origin(group, dx):
        return rows_of[group], wrap(x - dx, N_X)

    def along_x(dx, ch):
        xx = wrap(x + dx, N_X)
        return remote(
            grad_ref.at[:, columns(xx, ch)], gall.at[me, :, span(ch)],
            gxs.at[ch, dx - 1], gr.at[ch, dx, 0], here(y, xx, c),
        )

    def along_y(way, dx, ch):
        yy, xx = origin(0, dx)
        piece = gall.at[source(yy, xx, c), :, span(ch)]
        return remote(
            piece, piece, gys.at[ch, way, dx], gr.at[ch, (1 + way) * N_X + dx, 0],
            here(y_next if way == 0 else y_prev, x, c),
        )

    def onward(way, dx, ch):
        yy, xx = origin(1 + way, dx)
        piece = gall.at[source(yy, xx, c), parts[way], span(ch)]
        return remote(
            piece, piece, gyh.at[ch, way, dx], gr.at[ch, 3 * N_X + dx, way],
            here(y_next if way == 0 else y_prev, x, c),
        )

    def across(group, dx, ch):
        yy, xx = origin(group, dx)
        piece = gall.at[source(yy, xx, c), :, span(ch)]
        return remote(piece, piece, gcs.at[ch, group, dx], gcr.at[ch, group, dx], partner)

    def arrive(group, dx, ch):
        yy, xx = origin(group, dx)
        if group < 3:
            piece = gall.at[source(yy, xx, c), :, span(ch)]
            remote(piece, piece, gys.at[ch, 0, dx], gr.at[ch, group * N_X + dx, 0], partner).wait_recv()
        else:
            for part in range(2):
                piece = gall.at[source(yy, xx, c), parts[part], span(ch)]
                remote(piece, piece, gys.at[ch, 0, dx], gr.at[ch, 3 * N_X + dx, part], partner).wait_recv()

    def spread_own(dx, ch):
        along_y(0, dx, ch).start()
        along_y(1, dx, ch).start()
        across(0, dx, ch).start()

    def take_x(dx, ch):
        arrive(0, dx, ch)
        spread_own(dx, ch)

    def take_y(dx, ch):
        for way in range(2):
            arrive(1 + way, dx, ch)
            onward(way, dx, ch).start()
            across(1 + way, dx, ch).start()

    def take_far(dx, ch):
        arrive(3, dx, ch)
        across(3, dx, ch).start()

    def add_product(yy, xx, cc, ch):
        block = hall.at[xx, yy * N_C + cc]
        product = jnp.dot(
            block[pl.ds(0, rows), :], gall[source(yy, xx, cc), :, span(ch)], preferred_element_type=jnp.float32
        )
        flag = block[pl.ds(rows, FLAG_ROWS), :].astype(jnp.float32)[0:1, :]
        flag = jnp.concatenate([jnp.broadcast_to(flag, (rows, 128))] * (CHUNKS[ch][1] // 128), axis=1)
        host = xx * N_C + cc
        rounded = product.astype(jnp.bfloat16).astype(jnp.float32)
        prim[host, :, span(ch)] += jnp.where(flag > 0.5, 0.0, product)
        repl[host, :, span(ch)] += jnp.where(flag > 0.5, rounded, 0.0)

    def rail_product(group, dx, ch):
        add_product(*origin(group, dx), c, ch)

    def take_across(k, ch):
        group, dx = lax.div(k, N_X), lax.rem(k, N_X)
        dy = jnp.where(group == 1, N_Y - 1, jnp.where(group == 2, 1, jnp.where(group == 3, 2, 0)))
        yy, xx = wrap(y + dy, N_Y), wrap(x - dx, N_X)
        piece = gall.at[source(yy, xx, 1 - c), :, span(ch)]
        remote(piece, piece, gcs.at[ch, group, dx], gcr.at[ch, group, dx], partner).wait_recv()
        add_product(yy, xx, 1 - c, ch)

    h1 = []
    for k, (yy, cc) in enumerate(yc_peers):
        h1.append(remote(hid_ref.at[cc * N_Y + yy], hall.at[x, me8], hs1.at[k], hr1.at[k], here(yy, x, cc)))
        h1[-1].start()
    for dx in range(1, N_X):
        along_x(dx, 0).start()
    own_g.wait()
    spread_own(0, 0)
    prim[...] = jnp.zeros_like(prim)
    repl[...] = jnp.zeros_like(repl)
    own_h.wait()
    for copy in h1:
        copy.wait_recv()
    h2 = []
    for k, xx in enumerate(x_peers):
        h2.append(remote(hall.at[x], hall.at[x], hs2.at[k], hr2.at[k], here(y, xx, c)))
        h2[-1].start()
    for dx in range(1, N_X):
        along_x(dx, 1).start()
    loop(1, N_X - 1, lambda dx: take_x(dx, 0))
    loop(0, N_X, lambda dx: take_y(dx, 0))
    for copy in h2:
        copy.wait_recv()
    for group in range(3):
        loop(0, N_X, lambda dx, group=group: rail_product(group, dx, 0))

    def far_first(dx):
        take_far(dx, 0)
        rail_product(3, dx, 0)

    loop(0, N_X, far_first)
    loop(0, 4 * N_X, lambda k: take_across(k, 0))

    parity = lax.rem(z_lo, 2)

    def addend(e, part, ch):
        weight = jnp.where(lax.div(e, N_HOST) == parity, 1.0, 0.0)
        total = prim[lax.rem(e, N_HOST), part, span(ch)] * weight
        for h in range(N_HOST):
            weight = jnp.where(plan_ref[z_lo * N_HOST + h] == e, 1.0, 0.0)
            total += repl[h, part, span(ch)] * weight
        return total

    offset = [wrap(z - (8 * c + 2 * x + b), N_Z) for b in range(2)]
    lag = [jnp.where(r >= 8, r - 8, jnp.where(r == 0, 8, 7 - r)) for r in offset]

    def hop(e, ch, hf, r):
        way = jnp.where(r >= 8, 0, 1)
        piece = ring.at[way, e, pl.ds(hf * half, half), span(ch)]
        return remote(
            piece, piece, rs.at[ch, hf, e], rr.at[way, ch, hf, e], level(wrap(jnp.where(r >= 8, z + 1, z - 1), N_Z))
        )

    def landed(e, ch, hf, way):
        piece = ring.at[way, e, pl.ds(hf * half, half), span(ch)]
        remote(piece, piece, rs.at[ch, hf, e], rr.at[way, ch, hf, e], partner).wait_recv()

    def deliver(e, ch, hf):
        part = pl.ds(hf * half, half)
        xx, cc = lax.rem(lax.div(e, N_C), N_X), lax.rem(e, N_C)
        return remote(
            ring.at[0, e, part, span(ch)], out_ref.at[part, span(ch)], fs.at[ch, hf, e], fr.at[ch, hf], here(y, xx, cc)
        )

    def keep(e, ch, hf):
        part = pl.ds(hf * half, half)
        return pltpu.make_async_copy(ring.at[0, e, part, span(ch)], out_ref.at[part, span(ch)], fr.at[ch, hf])

    def mine(e):
        return lax.rem(e, N_HOST) == x * N_C + c

    def unit(e, ch, r):
        for hf in range(2):
            part = pl.ds(hf * half, half)
            way = jnp.where(r >= 8, 0, 1)

            @pl.when((r == 7) | (r == 8))
            def _():
                ring[way, e, part, span(ch)] = addend(e, part, ch)

            @pl.when((r != 7) & (r != 8) & (r != 0))
            def _():
                landed(e, ch, hf, way)
                ring[way, e, part, span(ch)] += addend(e, part, ch)

            @pl.when(r != 0)
            def _():
                hop(e, ch, hf, r).start()

            @pl.when(r == 0)
            def _():
                landed(e, ch, hf, 0)
                landed(e, ch, hf, 1)
                ring[0, e, part, span(ch)] += ring[1, e, part, span(ch)] + addend(e, part, ch)

                @pl.when(mine(e))
                def _():
                    keep(e, ch, hf).start()

                @pl.when(jnp.logical_not(mine(e)))
                def _():
                    deliver(e, ch, hf).start()

    def units(i):
        for ch in range(2):
            for b in range(2):
                first = EXPERTS * ch + N_HOST * b
                n = i - lag[b]

                @pl.when((n >= first) & (n < first + N_HOST))
                def _():
                    unit(n - EXPERTS * ch, ch, offset[b])


    def step_x(i):
        @pl.when(i > 0)
        def _():
            arrive(0, i, 1)

        spread_own(i, 1)
        rail_product(0, i, 1)
        units(i)

    def step_y(i):
        take_y(i - 4, 1)
        rail_product(1, i - 4, 1)
        rail_product(2, i - 4, 1)
        units(i)

    def step_far(i):
        take_far(i - 8, 1)
        rail_product(3, i - 8, 1)
        units(i)

    def step_across(i):
        loop(4 * (i - 12), 4, lambda k: take_across(k, 1))
        units(i)

    for first, step in ((0, step_x), (4, step_y), (8, step_far), (12, step_across)):
        loop(first, 4, step)
    loop(16, 2 * EXPERTS + 8 - 15, units)

    for copy in h1 + h2:
        copy.wait_send()
    for ch in range(2):
        def drain(dx, ch=ch):
            for way in range(2):
                along_y(way, dx, ch).wait_send()
                onward(way, dx, ch).wait_send()
            for group in range(4):
                across(group, dx, ch).wait_send()

        for dx in range(1, N_X):
            along_x(dx, ch).wait_send()
        loop(0, N_X, drain)

        def drain_units(e, ch=ch):
            b = lax.div(e, N_HOST)
            r = jnp.where(b == 0, offset[0], offset[1])
            for hf in range(2):
                @pl.when(r != 0)
                def _():
                    hop(e, ch, hf, r).wait_send()

                @pl.when((r == 0) & jnp.logical_not(mine(e)))
                def _():
                    deliver(e, ch, hf).wait_send()

        loop(0, EXPERTS, drain_units)
    kept = (x == lax.div(z_lo, 2)) & (c == z_hi)
    e_own = parity * N_HOST + x * N_C + c
    for ch in range(2):
        for hf in range(2):
            @pl.when(kept)
            def _():
                keep(e_own, ch, hf).wait()

            @pl.when(jnp.logical_not(kept))
            def _():
                deliver(e_own, ch, hf).wait_recv()


def weights_kernel(plan_ref, fresh_ref, out_ref, line, mixed, picked, own_sem, ls, lr, ms, mr, ps, pr):
    z_hi, z_lo, y, x, c = place()
    rows, width = fresh_ref.shape
    half = rows // 2

    def here(zz, xx, cc):
        return device(z_hi, zz, y, xx, cc)

    right, left = wrap(z_lo + 1, N_LO), wrap(z_lo - 1, N_LO)
    plane = [(dx, dc) for dx in range(N_X) for dc in range(N_C)]

    def peer(dx, dc):
        return wrap(x + dx, N_X), (c if dc == 0 else 1 - c)

    own = [
        pltpu.make_async_copy(fresh_ref.at[pl.ds(hf * half, half)], line.at[z_lo, hf], own_sem.at[3 + hf])
        for hf in range(2)
    ]
    for copy in own:
        copy.start()
    barrier = pltpu.get_barrier_semaphore()
    greeted = [here(z_lo, *peer(dx, dc)) for dx, dc in plane[1:]]
    greeted += [here(right, x, c), here(left, x, c)]
    for dev in greeted:
        pl.semaphore_signal(barrier, inc=1, device_id=dev, device_id_type=MESH)
    pl.semaphore_wait(barrier, len(greeted))
    for copy in own:
        copy.wait()

    def remote(src, dst, ssem, rsem, dev):
        return pltpu.make_async_remote_copy(
            src_ref=src, dst_ref=dst, send_sem=ssem, recv_sem=rsem,
            device_id=dev, device_id_type=MESH,
        )

    def line_copy(d, k, hf):
        piece = line.at[k, hf]
        return remote(piece, piece, ls.at[d, k, hf], lr.at[k, hf], here(right if d == 0 else left, x, c))

    def mix_copy(k, cc):
        q, b = lax.div(k, 2), lax.rem(k, 2)
        e = b * N_HOST + x * N_C + c
        dist = wrap(q - x, N_X)
        apart = jnp.where(cc == c, 0, 1)
        return remote(line.at[k, cc], mixed.at[e], ms.at[k, cc], mr.at[b, dist, apart], here(z_lo, q, cc))

    def local_mix(k):
        b = lax.rem(k, 2)
        return pltpu.make_async_copy(line.at[k, c], mixed.at[b * N_HOST + x * N_C + c], own_sem.at[1 + b])

    def scatter(k, cc):
        mine = (lax.div(k, 2) == x) & (cc == c)

        @pl.when(mine)
        def _():
            local_mix(k).start()

        @pl.when(jnp.logical_not(mine))
        def _():
            mix_copy(k, cc).start()

    for hf in range(2):
        @pl.when(z_lo < N_LO - 1)
        def _():
            line_copy(0, z_lo, hf).start()

        @pl.when(z_lo > 0)
        def _():
            line_copy(1, z_lo, hf).start()

    for hf in range(2):
        scatter(z_lo, hf)

    def line_step(t, carry):
        k, k2 = z_lo - t, z_lo + t
        for hf in range(2):
            @pl.when(k >= 0)
            def _():
                line_copy(0, k, hf).wait_recv()

                @pl.when(z_lo < N_LO - 1)
                def _():
                    line_copy(0, k, hf).start()

                scatter(k, hf)

            @pl.when(k2 < N_LO)
            def _():
                line_copy(1, k2, hf).wait_recv()

                @pl.when(z_lo > 0)
                def _():
                    line_copy(1, k2, hf).start()

                scatter(k2, hf)

        return carry

    lax.fori_loop(1, N_LO, line_step, 0)

    for b in range(2):
        local_mix(2 * x + b).wait()
        for dx, dc in plane[1:]:
            piece = mixed.at[0]
            remote(piece, piece, ms.at[0, 0], mr.at[b, dx, dc], here(z_lo, *peer(1, 0))).wait_recv()

    mine = out_ref.at[pl.ds(pl.multiple_of(c * half, 16), half), pl.ds(pl.multiple_of(x * width, 128), width)]
    sends = []
    for n, (dx, dc) in enumerate(plane):
        xx, cc = peer(dx, dc)
        picked[n] = mixed[plan_ref[z_lo * N_HOST + xx * N_C + cc]]
        if n == 0:
            sends.append(pltpu.make_async_copy(picked.at[0], mine, own_sem.at[0]))
        else:
            sends.append(remote(picked.at[n], mine, ps.at[n], pr.at[n], here(z_lo, xx, cc)))
        sends[-1].start()

    def drain(k, carry):
        for hf in range(2):
            @pl.when((z_lo < N_LO - 1) & (k <= z_lo))
            def _():
                line_copy(0, k, hf).wait_send()

            @pl.when((z_lo > 0) & (k >= z_lo))
            def _():
                line_copy(1, k, hf).wait_send()

            @pl.when(jnp.logical_not((lax.div(k, 2) == x) & (hf == c)))
            def _():
                mix_copy(k, hf).wait_send()

        return carry

    lax.fori_loop(0, N_LO, drain, 0)
    for copy in sends:
        copy.wait()


def per_device(
    hidden_rows, grad_rows, block_slot, live_rows, replica_plan, master, moment_one, moment_two
):
    hidden_units, tok = hidden_rows.shape
    model_width = grad_rows.shape[1]
    groups = N_HI * N_Y
    rows = hidden_units // groups
    width = model_width // QUART
    half = rows // 2
    kept = lax.iota(jnp.int32, tok) < live_rows[0]
    masked = jnp.where(kept[None, :], hidden_rows, jnp.zeros_like(hidden_rows)).reshape(groups, rows, tok)
    flags = jnp.broadcast_to((block_slot[0, 0] == 1).astype(jnp.bfloat16), (groups, FLAG_ROWS, tok))
    hid = jnp.concatenate([masked, flags], axis=1)
    dma = pltpu.SemaphoreType.DMA
    gradient = pl.pallas_call(
        gradient_kernel,
        out_shape=jax.ShapeDtypeStruct((rows, width), jnp.float32),
        in_specs=[
            pl.BlockSpec(memory_space=pltpu.SMEM),
            pl.BlockSpec(memory_space=pl.ANY),
            pl.BlockSpec(memory_space=pl.ANY),
        ],
        out_specs=pl.BlockSpec(memory_space=pltpu.VMEM),
        scratch_shapes=[
            pltpu.VMEM((N_X, N_Y * N_C, rows + FLAG_ROWS, tok), jnp.bfloat16),
            pltpu.VMEM((N_Y * N_X * N_C, tok, width), jnp.bfloat16),
            pltpu.VMEM((N_HOST, rows, width), jnp.float32),
            pltpu.VMEM((N_HOST, rows, width), jnp.float32),
            pltpu.VMEM((2, EXPERTS, rows, width), jnp.float32),
            dma((2,)), dma((7,)), dma((7,)), dma((3,)), dma((3,)),
            dma((2, 3)), dma((2, 4 * N_X, 2)), dma((2, 2, N_X)), dma((2, 2, N_X)), dma((2, 4, N_X)), dma((2, 4, N_X)),
            dma((2, 2, EXPERTS)), dma((2, 2, 2, EXPERTS)), dma((2, 2, EXPERTS)), dma((2, 2)),
        ],
        compiler_params=pltpu.CompilerParams(
            collective_id=0, has_side_effects=True, vmem_limit_bytes=40 * 2**20
        ),
        name="gradient",
    )(replica_plan, hid, grad_rows)
    weights_next, first_next, second_next = adam_update(
        master[0], moment_one[0], moment_two[0], gradient
    )
    fresh = weights_next.astype(jnp.bfloat16)
    replica_weight = pl.pallas_call(
        weights_kernel,
        out_shape=jax.ShapeDtypeStruct((rows, model_width), jnp.bfloat16),
        in_specs=[
            pl.BlockSpec(memory_space=pltpu.SMEM),
            pl.BlockSpec(memory_space=pltpu.VMEM),
        ],
        out_specs=pl.BlockSpec(memory_space=pltpu.VMEM),
        scratch_shapes=[
            pltpu.VMEM((N_LO, 2, half, width), jnp.bfloat16),
            pltpu.VMEM((EXPERTS, half, width), jnp.bfloat16),
            pltpu.VMEM((N_HOST, half, width), jnp.bfloat16),
            dma((5,)), dma((2, N_LO, 2)), dma((N_LO, 2)), dma((N_LO, N_C)), dma((2, N_X, N_C)),
            dma((N_HOST,)), dma((N_HOST,)),
        ],
        compiler_params=pltpu.CompilerParams(
            collective_id=1, has_side_effects=True, vmem_limit_bytes=16 * 2**20
        ),
        name="weights",
    )(replica_plan, fresh)
    return (weights_next[None], first_next[None], second_next[None], replica_weight[None])


def solution(mesh):
    return jax.shard_map(
        per_device,
        mesh=mesh,
        in_specs=(
            P(None, ("dp", "expert")),
            P(("dp", "expert"), None),
            P(("dp", "expert"), None),
            P(("dp", "expert")),
            P(),
            P("expert", "dp", None),
            P("expert", "dp", None),
            P("expert", "dp", None),
        ),
        out_specs=(
            P("expert", "dp", None),
            P("expert", "dp", None),
            P("expert", "dp", None),
            P("expert", "dp", None),
        ),
        check_vma=False,
    )
```

time: 988 us -> 174 us (0.18)
  waiting for transfers between devices: 641 us -> 0 us
  blocking collectives: 249 us -> 0 us
  Pallas kernels: 0 us -> 168 us
  local copies, waits for them, and re-layouts: 36.5 us -> 1.43 us
  starting transfers between devices: 25.1 us -> 0 us
  between operations: 15.6 us -> 2.08 us
    all_to_all x1 -> x0, waiting for transfers between devices: 276 us -> none  [per_device(): lax.all_to_all(summed, 'expert', split_axis=0, concat_axis=0, tiled=True)]
    psum x1 -> x0, waiting for transfers between devices: 262 us -> none  [per_device(): group_total = lax.psum(group_part, 'dp')]
    all_to_all x3 -> x0, blocking collectives: 249 us -> none  [the longest x1 191 us: per_device(): lax.all_to_all(sectioned, 'expert', split_axis=0, concat_axis=0, tiled=True)]
    pallas_call x0 -> x2, Pallas kernels: none -> 168 us  [the longest x1 105 us: per_device(): pl.pallas_call(gradient_kernel, out_shape=jax.ShapeDtypeStruct((rows, wid...]
    ppermute x3 -> x0, waiting for transfers between devices: 103 us -> none  [from_behind(): return lax.ppermute(block, axis, route)]
    ppermute x3 -> x0, starting transfers between devices: 16.4 us -> none  [from_behind(): return lax.ppermute(block, axis, route)]
    dynamic_slice x5 -> x0, local copies, waits for them, and re-layouts: 14.7 us -> none  [the longest x3 8.63 us: per_device(): piece = lax.dynamic_index_in_dim(primary_part, target, 1, False)]
    reshape x6 -> x0, local copies, waits for them, and re-layouts: 13.2 us -> none  [the longest x1 7.61 us: per_device(): replica_terms.reshape(expert_count, hidden_units // expert_count, QUART,...]
  transfers between devices with their start and end apart: 5 -> 0, of which waited for: 3 -> 0; matrix products, arithmetic and copies ran while one was open for 2% -> 0% of each run, Pallas kernels for 0% -> 0%
where the time goes in v2:
time: 174 us
  Pallas kernels  168 us (97%)
  between operations  2.08 us (1%)
  other arithmetic  1.93 us (1%)
    pallas_call x1, Pallas kernels, per_device(): pl.pallas_call(gradient_kernel, out_shape=jax.ShapeDtypeStruct((rows, wid...  105 us
    pallas_call x1, Pallas kernels, per_device(): pl.pallas_call(weights_kernel, out_shape=jax.ShapeDtypeStruct((rows, mode...  63.1 us

profile of v2, /device:TPU:1, one launch (start us, length us, event | category | flops | bytes accessed | tf_op | source)
XLA Modules:
  0.0 173.8 jit_solution(2137424928321208765)
XLA Ops:
  0.6 0.0 copy-start
  2.0 0.9 broadcast_select_fusion
  3.0 0.0 copy-start.1
  3.0 0.0 copy-done
  3.0 0.6 copy-done.1
  3.6 0.0 copy-start.2
  3.6 0.0 copy-start.3
  3.6 0.0 copy-start.4
  3.6 105.3 %gradient.1 = f32[96,640]{1,0:T(8,128)S(1)} custom-call(s32[64]{0:T(128)S(1)} %copy-done.1, bf16[8,112,128]{2,1,0:T(8,128)(2,1)S(1)} %concatenate.3.hid_ref, bf16[128,2560]{1,0:T(8,128)(2,1)S(1)} %copy-done), custom_call_target="tpu_custom_call" | custom-call | tf_op jit(solution)/shard_map/gradient/pallas_call | solution.py:538
  108.9 0.0 copy-done.2
  108.9 0.0 copy-done.3
  109.0 0.0 copy-done.4
  109.0 1.0 fusion.5
  109.9 63.1 %weights.1 = bf16[96,2560]{1,0:T(8,128)(2,1)S(1)} custom-call(s32[64]{0:T(128)S(1)} %copy-done.1, bf16[96,640]{1,0:T(8,128)(2,1)S(1)} %get-tuple-element.4.fresh_ref), custom_call_target="tpu_custom_call" | custom-call | tf_op jit(solution)/shard_map/weights/pallas_call | solution.py:566
  173.1 0.8 copy.15
  (2 shorter events, 0.0 us)
Async XLA Ops:
  0.6 2.4 %copy-start = (bf16[128,2560]{1,0:T(8,128)(2,1)S(1)}, bf16[128,2560]{1,0:T(8,128)(2,1)}, u32[]{:S(2)}) copy-start(bf16[128,2560]{1,0:T(8,128)(2,1)} %grad_ref.1) | copy-start | bytes 1966084
  3.0 0.7 copy-start.1
  3.6 105.3 %copy-start.2 = (f32[1,96,640]{2,1,0:T(8,128)S(1)}, f32[1,96,640]{2,1,0:T(8,128)}, u32[]{:S(2)}) copy-start(f32[1,96,640]{2,1,0:T(8,128)} %param.15) | copy-start | bytes 737284
  3.6 105.3 %copy-start.3 = (f32[1,96,640]{2,1,0:T(8,128)S(1)}, f32[1,96,640]{2,1,0:T(8,128)}, u32[]{:S(2)}) copy-start(f32[1,96,640]{2,1,0:T(8,128)} %param.14) | copy-start | bytes 737284
  3.6 105.3 %copy-start.4 = (f32[1,96,640]{2,1,0:T(8,128)S(1)}, f32[1,96,640]{2,1,0:T(8,128)}, u32[]{:S(2)}) copy-start(f32[1,96,640]{2,1,0:T(8,128)} %param.13) | copy-start | bytes 737284

commit v3 on v2

--- a/solution.py
+++ b/solution.py
@@ -15,6 +15,10 @@
 QUART = 4
 EXPERTS = 16
 FLAG_ROWS = 16
+VMEM_BYTES = 67043328
+HOP_LAG = 3
+STEPS = 32000.0
+FINE = 65536.0
 CHUNKS = ((0, 384), (384, 256))
 
 beta_one = 0.9
@@ -51,14 +55,16 @@
     return lax.rem(v + n, n)
 
 
-def gradient_kernel(
-    plan_ref, hid_ref, grad_ref, out_ref,
-    hall, gall, prim, repl, ring,
+def step_kernel(
+    plan_ref, hid_ref, grad_ref, master_ref, first_ref, second_ref,
+    total, out_ref,
+    hall, gall, prim, repl, ring_a, ring_b, done, state, line, mixed_a, mixed_b, picked,
     own_sem, hs1, hr1, hs2, hr2, gxs, gr, gys, gyh, gcs, gcr, rs, rr, fs, fr,
+    ls, lr, ms, mr, lm, ps, pr,
 ):
     z_hi, z_lo, y, x, c = place()
     z = z_hi * N_LO + z_lo
-    rows, width = out_ref.shape
+    rows, width = master_ref.shape
     half = rows // 2
     tok = grad_ref.shape[0]
 
@@ -94,6 +100,12 @@
     own_h = pltpu.make_async_copy(hid_ref.at[c * N_Y + y], hall.at[x, me8], own_sem.at[1])
     own_h.start()
     own_g.start()
+    loads = [
+        pltpu.make_async_copy(ref, state.at[n], own_sem.at[2 + n])
+        for n, ref in enumerate((master_ref, first_ref, second_ref))
+    ]
+    for copy in loads:
+        copy.start()
 
     barrier = pltpu.get_barrier_semaphore()
     greeted = [here(yy, x, cc) for yy, cc in yc_peers] + [here(y, xx, cc) for xx, cc in xc_peers]
@@ -245,29 +257,67 @@
         return total
 
     offset = [wrap(z - (8 * c + 2 * x + b), N_Z) for b in range(2)]
-    lag = [jnp.where(r >= 8, r - 8, jnp.where(r == 0, 8, 7 - r)) for r in offset]
+    lag = [HOP_LAG * jnp.where(r >= 8, r - 8, jnp.where(r == 0, 8, 7 - r)) for r in offset]
+
+    rings = (ring_a, ring_b)
+    groups = half // 8
+    pairs = groups // 2
+    lanes = lax.shift_right_logical(lax.broadcasted_iota(jnp.int32, (8, 128), 1), 4)
+
+    def slab(e, ch, hf, way):
+        return rings[ch].at[way, e, hf]
+
+    def encode(value, ref, ch):
+        tiles = CHUNKS[ch][1] // 128
+        top = jnp.zeros((8, 128), jnp.float32)
+        for g in range(groups):
+            top = jnp.where(lanes == g, jnp.max(jnp.abs(value[8 * g:8 * g + 8]), axis=1, keepdims=True), top)
+        level_of = jnp.ceil(jnp.log2(jnp.maximum(top, 1e-30)) * FINE).astype(jnp.int32) + 64
+        factor = jnp.exp2(level_of.astype(jnp.float32) * (-1.0 / FINE)) * STEPS
+        whole = [
+            jnp.round(value[8 * g:8 * g + 8] * factor[:, 16 * g:16 * g + 1]).astype(jnp.int32) for g in range(groups)
+        ]
+        for g in range(pairs):
+            word = (whole[g] << 16) | (whole[g + pairs] & 0xFFFF)
+            for t in range(tiles):
+                ref[g * tiles + t] = word[:, 128 * t:128 * t + 128]
+        ref[pairs * tiles] = level_of
+
+    def decode(ref, ch):
+        tiles = CHUNKS[ch][1] // 128
+        factor = jnp.exp2(ref[pairs * tiles].astype(jnp.float32) * (1.0 / FINE)) * (1.0 / STEPS)
+        upper, lower = [], []
+        for g in range(pairs):
+            word = jnp.concatenate([ref[g * tiles + t] for t in range(tiles)], axis=1)
+            upper.append((word >> 16).astype(jnp.float32) * factor[:, 16 * g:16 * g + 1])
+            k = 16 * (g + pairs)
+            lower.append(((word << 16) >> 16).astype(jnp.float32) * factor[:, k:k + 1])
+        return jnp.concatenate(upper + lower, axis=0)
 
     def hop(e, ch, hf, r):
         way = jnp.where(r >= 8, 0, 1)
-        piece = ring.at[way, e, pl.ds(hf * half, half), span(ch)]
+        piece = slab(e, ch, hf, way)
         return remote(
             piece, piece, rs.at[ch, hf, e], rr.at[way, ch, hf, e], level(wrap(jnp.where(r >= 8, z + 1, z - 1), N_Z))
         )
 
     def landed(e, ch, hf, way):
-        piece = ring.at[way, e, pl.ds(hf * half, half), span(ch)]
+        piece = slab(e, ch, hf, way)
         remote(piece, piece, rs.at[ch, hf, e], rr.at[way, ch, hf, e], partner).wait_recv()
 
     def deliver(e, ch, hf):
         part = pl.ds(hf * half, half)
         xx, cc = lax.rem(lax.div(e, N_C), N_X), lax.rem(e, N_C)
         return remote(
-            ring.at[0, e, part, span(ch)], out_ref.at[part, span(ch)], fs.at[ch, hf, e], fr.at[ch, hf], here(y, xx, cc)
+            done.at[lax.rem(e, N_HOST), part, span(ch)], total.at[part, span(ch)],
+            fs.at[ch, hf, e], fr.at[ch, hf], here(y, xx, cc),
         )
 
     def keep(e, ch, hf):
         part = pl.ds(hf * half, half)
-        return pltpu.make_async_copy(ring.at[0, e, part, span(ch)], out_ref.at[part, span(ch)], fr.at[ch, hf])
+        return pltpu.make_async_copy(
+            done.at[lax.rem(e, N_HOST), part, span(ch)], total.at[part, span(ch)], fr.at[ch, hf]
+        )
 
     def mine(e):
         return lax.rem(e, N_HOST) == x * N_C + c
@@ -279,12 +329,13 @@
 
             @pl.when((r == 7) | (r == 8))
             def _():
-                ring[way, e, part, span(ch)] = addend(e, part, ch)
+                encode(addend(e, part, ch), slab(e, ch, hf, way), ch)
 
             @pl.when((r != 7) & (r != 8) & (r != 0))
             def _():
+                own = addend(e, part, ch)
                 landed(e, ch, hf, way)
-                ring[way, e, part, span(ch)] += addend(e, part, ch)
+                encode(own + decode(slab(e, ch, hf, way), ch), slab(e, ch, hf, way), ch)
 
             @pl.when(r != 0)
             def _():
@@ -292,9 +343,12 @@
 
             @pl.when(r == 0)
             def _():
+                own = addend(e, part, ch)
                 landed(e, ch, hf, 0)
                 landed(e, ch, hf, 1)
-                ring[0, e, part, span(ch)] += ring[1, e, part, span(ch)] + addend(e, part, ch)
+                done[lax.rem(e, N_HOST), part, span(ch)] = (
+                    own + decode(slab(e, ch, hf, 0), ch) + decode(slab(e, ch, hf, 1), ch)
+                )
 
                 @pl.when(mine(e))
                 def _():
@@ -314,6 +368,116 @@
                 def _():
                     unit(n - EXPERTS * ch, ch, offset[b])
 
+    kept = (x == lax.div(z_lo, 2)) & (c == z_hi)
+    e_own = parity * N_HOST + x * N_C + c
+
+    def adam(ch):
+        for hf in range(2):
+            @pl.when(kept)
+            def _():
+                keep(e_own, ch, hf).wait()
+
+            @pl.when(jnp.logical_not(kept))
+            def _():
+                deliver(e_own, ch, hf).wait_recv()
+
+            part = pl.ds(hf * half, half)
+            weights_next = adam_update(
+                state[0, part, span(ch)], state[1, part, span(ch)], state[2, part, span(ch)], total[part, span(ch)]
+            )[0]
+            line[z_lo, hf, :, span(ch)] = weights_next.astype(jnp.bfloat16)
+
+    def line_copy(d, k, hf, ch):
+        piece = line.at[k, hf, :, span(ch)]
+        dev = level(wrap(z + 1, N_Z) if d == 0 else wrap(z - 1, N_Z))
+        return remote(piece, piece, ls.at[ch, d, k, hf], lr.at[ch, k, hf], dev)
+
+    mixed = (mixed_a, mixed_b)
+
+    def mix_copy(k, cc, ch):
+        q, b = lax.div(k, 2), lax.rem(k, 2)
+        e = b * N_HOST + x * N_C + c
+        dist = wrap(q - x, N_X)
+        apart = jnp.where(cc == c, 0, 1)
+        return remote(
+            line.at[k, cc, :, span(ch)], mixed[ch].at[e], ms.at[ch, k, cc], mr.at[ch, b, dist, apart],
+            here(y, q, cc),
+        )
+
+    def local_mix(k, ch):
+        b = lax.rem(k, 2)
+        return pltpu.make_async_copy(
+            line.at[k, c, :, span(ch)], mixed[ch].at[b * N_HOST + x * N_C + c], lm.at[ch, b]
+        )
+
+    def scatter(k, cc, ch):
+        same = (lax.div(k, 2) == x) & (cc == c)
+
+        @pl.when(same)
+        def _():
+            local_mix(k, ch).start()
+
+        @pl.when(jnp.logical_not(same))
+        def _():
+            mix_copy(k, cc, ch).start()
+
+    def line_start(ch):
+        for hf in range(2):
+            @pl.when(z_lo < N_LO - 1)
+            def _():
+                line_copy(0, z_lo, hf, ch).start()
+
+            @pl.when(z_lo > 0)
+            def _():
+                line_copy(1, z_lo, hf, ch).start()
+
+        for hf in range(2):
+            scatter(z_lo, hf, ch)
+
+    def line_step(t, ch):
+        k, k2 = z_lo - t, z_lo + t
+        for hf in range(2):
+            @pl.when(k >= 0)
+            def _():
+                line_copy(0, k, hf, ch).wait_recv()
+
+                @pl.when(z_lo < N_LO - 1)
+                def _():
+                    line_copy(0, k, hf, ch).start()
+
+                scatter(k, hf, ch)
+
+            @pl.when(k2 < N_LO)
+            def _():
+                line_copy(1, k2, hf, ch).wait_recv()
+
+                @pl.when(z_lo > 0)
+                def _():
+                    line_copy(1, k2, hf, ch).start()
+
+                scatter(k2, hf, ch)
+
+    plane = [(dx, dc) for dx in range(N_X) for dc in range(N_C)]
+
+    def pick_copy(n, ch):
+        dx, dc = plane[n]
+        target = out_ref.at[pl.ds(pl.multiple_of(c * half, 16), half), columns(x, ch)]
+        piece = picked.at[n, :, span(ch)]
+        if n == 0:
+            return pltpu.make_async_copy(piece, target, pr.at[ch, 0])
+        return remote(piece, target, ps.at[ch, n], pr.at[ch, n], here(y, wrap(x + dx, N_X), c if dc == 0 else 1 - c))
+
+    def pick(ch):
+        for b in range(2):
+            local_mix(2 * x + b, ch).wait()
+            for dx, dc in plane[1:]:
+                piece = mixed[ch].at[0]
+                remote(piece, piece, ms.at[ch, 0, 0], mr.at[ch, b, dx, dc], partner).wait_recv()
+        for n, (dx, dc) in enumerate(plane):
+            xx, cc = wrap(x + dx, N_X), (c if dc == 0 else 1 - c)
+            picked[n, :, span(ch)] = mixed[ch][plan_ref[z_lo * N_HOST + xx * N_C + cc]]
+            pick_copy(n, ch).start()
+
 
     def step_x(i):
         @pl.when(i > 0)
@@ -341,7 +505,26 @@
 
     for first, step in ((0, step_x), (4, step_y), (8, step_far), (12, step_across)):
         loop(first, 4, step)
-    loop(16, 2 * EXPERTS + 8 - 15, units)
+    filled = 8 * HOP_LAG
+    loop(16, filled, units)
+    for copy in loads:
+        copy.wait()
+    adam(0)
+    line_start(0)
+
+    def step_line(t):
+        units(filled + 14 + 2 * t)
+        line_step(t, 0)
+        units(filled + 15 + 2 * t)
+
+    loop(1, N_LO - 1, step_line)
+    loop(filled + 30, 2, units)
+    adam(1)
+    line_start(1)
+    line_step(1, 1)
+    pick(0)
+    loop(2, N_LO - 2, lambda t: line_step(t, 1))
+    pick(1)
 
     for copy in h1 + h2:
         copy.wait_send()
@@ -370,155 +553,24 @@
                     deliver(e, ch, hf).wait_send()
 
         loop(0, EXPERTS, drain_units)
-    kept = (x == lax.div(z_lo, 2)) & (c == z_hi)
-    e_own = parity * N_HOST + x * N_C + c
     for ch in range(2):
-        for hf in range(2):
-            @pl.when(kept)
-            def _():
-                keep(e_own, ch, hf).wait()
-
-            @pl.when(jnp.logical_not(kept))
-            def _():
-                deliver(e_own, ch, hf).wait_recv()
-
-
-def weights_kernel(plan_ref, fresh_ref, out_ref, line, mixed, picked, own_sem, ls, lr, ms, mr, ps, pr):
-    z_hi, z_lo, y, x, c = place()
-    rows, width = fresh_ref.shape
-    half = rows // 2
-
-    def here(zz, xx, cc):
-        return device(z_hi, zz, y, xx, cc)
-
-    right, left = wrap(z_lo + 1, N_LO), wrap(z_lo - 1, N_LO)
-    plane = [(dx, dc) for dx in range(N_X) for dc in range(N_C)]
-
-    def peer(dx, dc):
-        return wrap(x + dx, N_X), (c if dc == 0 else 1 - c)
-
-    own = [
-        pltpu.make_async_copy(fresh_ref.at[pl.ds(hf * half, half)], line.at[z_lo, hf], own_sem.at[3 + hf])
-        for hf in range(2)
-    ]
-    for copy in own:
-        copy.start()
-    barrier = pltpu.get_barrier_semaphore()
-    greeted = [here(z_lo, *peer(dx, dc)) for dx, dc in plane[1:]]
-    greeted += [here(right, x, c), here(left, x, c)]
-    for dev in greeted:
-        pl.semaphore_signal(barrier, inc=1, device_id=dev, device_id_type=MESH)
-    pl.semaphore_wait(barrier, len(greeted))
-    for copy in own:
-        copy.wait()
-
-    def remote(src, dst, ssem, rsem, dev):
-        return pltpu.make_async_remote_copy(
-            src_ref=src, dst_ref=dst, send_sem=ssem, recv_sem=rsem,
-            device_id=dev, device_id_type=MESH,
-        )
-
-    def line_copy(d, k, hf):
-        piece = line.at[k, hf]
-        return remote(piece, piece, ls.at[d, k, hf], lr.at[k, hf], here(right if d == 0 else left, x, c))
-
-    def mix_copy(k, cc):
-        q, b = lax.div(k, 2), lax.rem(k, 2)
-        e = b * N_HOST + x * N_C + c
-        dist = wrap(q - x, N_X)
-        apart = jnp.where(cc == c, 0, 1)
-        return remote(line.at[k, cc], mixed.at[e], ms.at[k, cc], mr.at[b, dist, apart], here(z_lo, q, cc))
-
-    def local_mix(k):
-        b = lax.rem(k, 2)
-        return pltpu.make_async_copy(line.at[k, c], mixed.at[b * N_HOST + x * N_C + c], own_sem.at[1 + b])
-
-    def scatter(k, cc):
-        mine = (lax.div(k, 2) == x) & (cc == c)
-
-        @pl.when(mine)
-        def _():
-            local_mix(k).start()
-
-        @pl.when(jnp.logical_not(mine))
-        def _():
-            mix_copy(k, cc).start()
-
-    for hf in range(2):
-        @pl.when(z_lo < N_LO - 1)
-        def _():
-            line_copy(0, z_lo, hf).start()
-
-        @pl.when(z_lo > 0)
-        def _():
-            line_copy(1, z_lo, hf).start()
-
-    for hf in range(2):
-        scatter(z_lo, hf)
-
-    def line_step(t, carry):
-        k, k2 = z_lo - t, z_lo + t
-        for hf in range(2):
-            @pl.when(k >= 0)
-            def _():
-                line_copy(0, k, hf).wait_recv()
-
-                @pl.when(z_lo < N_LO - 1)
-                def _():
-                    line_copy(0, k, hf).start()
-
-                scatter(k, hf)
-
-            @pl.when(k2 < N_LO)
-            def _():
-                line_copy(1, k2, hf).wait_recv()
-
-                @pl.when(z_lo > 0)
-                def _():
-                    line_copy(1, k2, hf).start()
-
-                scatter(k2, hf)
-
-        return carry
-
-    lax.fori_loop(1, N_LO, line_step, 0)
-
-    for b in range(2):
-        local_mix(2 * x + b).wait()
-        for dx, dc in plane[1:]:
-            piece = mixed.at[0]
-            remote(piece, piece, ms.at[0, 0], mr.at[b, dx, dc], here(z_lo, *peer(1, 0))).wait_recv()
-
-    mine = out_ref.at[pl.ds(pl.multiple_of(c * half, 16), half), pl.ds(pl.multiple_of(x * width, 128), width)]
-    sends = []
-    for n, (dx, dc) in enumerate(plane):
-        xx, cc = peer(dx, dc)
-        picked[n] = mixed[plan_ref[z_lo * N_HOST + xx * N_C + cc]]
-        if n == 0:
-            sends.append(pltpu.make_async_copy(picked.at[0], mine, own_sem.at[0]))
-        else:
-            sends.append(remote(picked.at[n], mine, ps.at[n], pr.at[n], here(z_lo, xx, cc)))
-        sends[-1].start()
-
-    def drain(k, carry):
-        for hf in range(2):
-            @pl.when((z_lo < N_LO - 1) & (k <= z_lo))
-            def _():
-                line_copy(0, k, hf).wait_send()
-
-            @pl.when((z_lo > 0) & (k >= z_lo))
-            def _():
-                line_copy(1, k, hf).wait_send()
-
-            @pl.when(jnp.logical_not((lax.div(k, 2) == x) & (hf == c)))
-            def _():
-                mix_copy(k, hf).wait_send()
-
-        return carry
-
-    lax.fori_loop(0, N_LO, drain, 0)
-    for copy in sends:
-        copy.wait()
+        def drain_line(k, ch=ch):
+            for hf in range(2):
+                @pl.when((z_lo < N_LO - 1) & (k <= z_lo))
+                def _():
+                    line_copy(0, k, hf, ch).wait_send()
+
+                @pl.when((z_lo > 0) & (k >= z_lo))
+                def _():
+                    line_copy(1, k, hf, ch).wait_send()
+
+                @pl.when(jnp.logical_not((lax.div(k, 2) == x) & (hf == c)))
+                def _():
+                    mix_copy(k, hf, ch).wait_send()
+
+        loop(0, N_LO, drain_line)
+        for n in range(N_HOST):
+            pick_copy(n, ch).wait()
 
 
 def per_device(
@@ -535,54 +587,38 @@
     flags = jnp.broadcast_to((block_slot[0, 0] == 1).astype(jnp.bfloat16), (groups, FLAG_ROWS, tok))
     hid = jnp.concatenate([masked, flags], axis=1)
     dma = pltpu.SemaphoreType.DMA
-    gradient = pl.pallas_call(
-        gradient_kernel,
-        out_shape=jax.ShapeDtypeStruct((rows, width), jnp.float32),
-        in_specs=[
-            pl.BlockSpec(memory_space=pltpu.SMEM),
-            pl.BlockSpec(memory_space=pl.ANY),
-            pl.BlockSpec(memory_space=pl.ANY),
-        ],
-        out_specs=pl.BlockSpec(memory_space=pltpu.VMEM),
+    share = jax.ShapeDtypeStruct((rows, width), jnp.float32)
+    hbm, vmem = pl.BlockSpec(memory_space=pltpu.HBM), pl.BlockSpec(memory_space=pltpu.VMEM)
+    gradient, replica_weight = pl.pallas_call(
+        step_kernel,
+        out_shape=(share, jax.ShapeDtypeStruct((rows, model_width), jnp.bfloat16)),
+        in_specs=[pl.BlockSpec(memory_space=pltpu.SMEM)] + [hbm] * 5,
+        out_specs=(vmem,) * 2,
         scratch_shapes=[
             pltpu.VMEM((N_X, N_Y * N_C, rows + FLAG_ROWS, tok), jnp.bfloat16),
             pltpu.VMEM((N_Y * N_X * N_C, tok, width), jnp.bfloat16),
             pltpu.VMEM((N_HOST, rows, width), jnp.float32),
             pltpu.VMEM((N_HOST, rows, width), jnp.float32),
-            pltpu.VMEM((2, EXPERTS, rows, width), jnp.float32),
-            dma((2,)), dma((7,)), dma((7,)), dma((3,)), dma((3,)),
+            pltpu.VMEM((2, EXPERTS, 2, half // 16 * (CHUNKS[0][1] // 128) + 1, 8, 128), jnp.int32),
+            pltpu.VMEM((2, EXPERTS, 2, half // 16 * (CHUNKS[1][1] // 128) + 1, 8, 128), jnp.int32),
+            pltpu.VMEM((N_HOST, rows, width), jnp.float32),
+            pltpu.VMEM((3, rows, width), jnp.float32),
+            pltpu.VMEM((N_LO, 2, half, width), jnp.bfloat16),
+            pltpu.VMEM((EXPERTS, half, CHUNKS[0][1]), jnp.bfloat16),
+            pltpu.VMEM((EXPERTS, half, CHUNKS[1][1]), jnp.bfloat16),
+            pltpu.VMEM((N_HOST, half, width), jnp.bfloat16),
+            dma((5,)), dma((7,)), dma((7,)), dma((3,)), dma((3,)),
             dma((2, 3)), dma((2, 4 * N_X, 2)), dma((2, 2, N_X)), dma((2, 2, N_X)), dma((2, 4, N_X)), dma((2, 4, N_X)),
             dma((2, 2, EXPERTS)), dma((2, 2, 2, EXPERTS)), dma((2, 2, EXPERTS)), dma((2, 2)),
+            dma((2, 2, N_LO, 2)), dma((2, N_LO, 2)), dma((2, N_LO, N_C)), dma((2, 2, N_X, N_C)), dma((2, 2)),
+            dma((2, N_HOST)), dma((2, N_HOST)),
         ],
         compiler_params=pltpu.CompilerParams(
-            collective_id=0, has_side_effects=True, vmem_limit_bytes=40 * 2**20
+            collective_id=0, has_side_effects=True, vmem_limit_bytes=VMEM_BYTES
         ),
-        name="gradient",
-    )(replica_plan, hid, grad_rows)
-    weights_next, first_next, second_next = adam_update(
-        master[0], moment_one[0], moment_two[0], gradient
-    )
-    fresh = weights_next.astype(jnp.bfloat16)
-    replica_weight = pl.pallas_call(
-        weights_kernel,
-        out_shape=jax.ShapeDtypeStruct((rows, model_width), jnp.bfloat16),
-        in_specs=[
-            pl.BlockSpec(memory_space=pltpu.SMEM),
-            pl.BlockSpec(memory_space=pltpu.VMEM),
-        ],
-        out_specs=pl.BlockSpec(memory_space=pltpu.VMEM),
-        scratch_shapes=[
-            pltpu.VMEM((N_LO, 2, half, width), jnp.bfloat16),
-            pltpu.VMEM((EXPERTS, half, width), jnp.bfloat16),
-            pltpu.VMEM((N_HOST, half, width), jnp.bfloat16),
-            dma((5,)), dma((2, N_LO, 2)), dma((N_LO, 2)), dma((N_LO, N_C)), dma((2, N_X, N_C)),
-            dma((N_HOST,)), dma((N_HOST,)),
-        ],
-        compiler_params=pltpu.CompilerParams(
-            collective_id=1, has_side_effects=True, vmem_limit_bytes=16 * 2**20
-        ),
-        name="weights",
-    )(replica_plan, fresh)
+        name="step",
+    )(replica_plan, hid, grad_rows, master[0], moment_one[0], moment_two[0])
+    weights_next, first_next, second_next = adam_update(master[0], moment_one[0], moment_two[0], gradient)
     return (weights_next[None], first_next[None], second_next[None], replica_weight[None])
 
 

time: 174 us -> 157 us (0.902)
  Pallas kernels: 168 us -> 150 us
    pallas_call x2 -> x1, Pallas kernels: 168 us -> 150 us  [per_device(): pl.pallas_call(step_kernel, out_shape=(share, jax.ShapeDtypeStruct((rows,...]
    broadcast_in_dim x0 -> x1, other arithmetic: none -> 2.39 us  [per_device(): second_next[None]]
where the time goes in v3:
time: 157 us
  Pallas kernels  150 us (96%)
  other arithmetic  3.34 us (2%)
  between operations  1.96 us (1%)
    pallas_call x1, Pallas kernels, per_device(): pl.pallas_call(step_kernel, out_shape=(share, jax.ShapeDtypeStruct((rows,...  150 us

profile of v3, /device:TPU:1, one launch (start us, length us, event | category | flops | bytes accessed | tf_op | source)
XLA Modules:
  0.0 156.7 jit_solution(16669625759181250513)
XLA Ops:
  1.9 0.9 broadcast_select_fusion
  2.9 0.7 concatenate.3.hid_ref
  3.6 149.9 %step.1 = (f32[96,640]{1,0:T(8,128)}, bf16[96,2560]{1,0:T(8,128)(2,1)}) custom-call(s32[64]{0:T(128)} %plan_ref.1, bf16[8,112,128]{2,1,0:T(8,128)(2,1)} %concatenate.3.hid_ref, bf16[128,2560]{1,0:T(8,128)(2,1)} %grad_ref.1, f32[96,640]{1,0:T(8,128)} %bitcast.19, f32[96,640]{1,0:T(8,128)} %bitcast.20, f32[96,640]{1,0:T(8,128)} %bitcast.21), custom_call_target="tpu_custom_call" | custom-call | tf_op jit(solution)/shard_map/step/pallas_call | solution.py:592
  153.5 0.0 copy-start
  153.5 2.4 %fusion.2 = (f32[1,96,640]{2,1,0:T(8,128)}, f32[1,96,640]{2,1,0:T(8,128)}, f32[1,96,640]{2,1,0:T(8,128)}) fusion(f32[96,640]{1,0:T(8,128)} %get-tuple-element.6, f32[1,96,640]{2,1,0:T(8,128)} %param.15, f32[1,96,640]{2,1,0:T(8,128)} %param.14, f32[1,96,640]{2,1,0:T(8,128)} %param.13), kind=kLoop, calls=%fused_computation.6 | loop fusion | flops 921600 | bytes 1720320 | tf_op jit(solution)/shard_map/broadcast_in_dim | solution.py:622
  155.9 0.0 copy-done
  155.9 0.8 copy.15
  (1 shorter events, 0.0 us)
Async XLA Ops:
  153.5 2.4 %copy-start = (bf16[96,2560]{1,0:T(8,128)(2,1)S(1)}, bf16[96,2560]{1,0:T(8,128)(2,1)}, u32[]{:S(2)}) copy-start(bf16[96,2560]{1,0:T(8,128)(2,1)} %get-tuple-element.7) | copy-start | bytes 1474564

commit v4 on v3

--- a/solution.py
+++ b/solution.py
@@ -16,7 +16,7 @@
 EXPERTS = 16
 FLAG_ROWS = 16
 VMEM_BYTES = 67043328
-HOP_LAG = 3
+HOP_LAG = 4
 STEPS = 32000.0
 FINE = 65536.0
 CHUNKS = ((0, 384), (384, 256))
@@ -232,8 +232,11 @@
         h2[-1].start()
     for dx in range(1, N_X):
         along_x(dx, 1).start()
-    loop(1, N_X - 1, lambda dx: take_x(dx, 0))
-    loop(0, N_X, lambda dx: take_y(dx, 0))
+    def nearest(k):
+        return jnp.where(k == 2, 3, jnp.where(k == 3, 2, k))
+
+    loop(1, N_X - 1, lambda k: take_x(nearest(k), 0))
+    loop(0, N_X, lambda k: take_y(nearest(k), 0))
     for copy in h2:
         copy.wait_recv()
     for group in range(3):

time: 157 us -> 158 us (level)
  no operation moved by 1% of the time
where the time goes in v4:
time: 158 us
  Pallas kernels  151 us (96%)
  other arithmetic  3.34 us (2%)
  between operations  1.96 us (1%)
    pallas_call x1, Pallas kernels, per_device(): pl.pallas_call(step_kernel, out_shape=(share, jax.ShapeDtypeStruct((rows,...  151 us

profile of v4, /device:TPU:1, one launch (start us, length us, event | category | flops | bytes accessed | tf_op | source)
XLA Modules:
  0.0 158.2 jit_solution(2210516176674789533)
XLA Ops:
  1.9 0.9 broadcast_select_fusion
  2.9 0.7 concatenate.3.hid_ref
  3.6 151.4 %step.1 = (f32[96,640]{1,0:T(8,128)}, bf16[96,2560]{1,0:T(8,128)(2,1)}) custom-call(s32[64]{0:T(128)} %plan_ref.1, bf16[8,112,128]{2,1,0:T(8,128)(2,1)} %concatenate.3.hid_ref, bf16[128,2560]{1,0:T(8,128)(2,1)} %grad_ref.1, f32[96,640]{1,0:T(8,128)} %bitcast.19, f32[96,640]{1,0:T(8,128)} %bitcast.20, f32[96,640]{1,0:T(8,128)} %bitcast.21), custom_call_target="tpu_custom_call" | custom-call | tf_op jit(solution)/shard_map/step/pallas_call | solution.py:595
  155.0 0.0 copy-start
  155.0 2.4 %fusion.2 = (f32[1,96,640]{2,1,0:T(8,128)}, f32[1,96,640]{2,1,0:T(8,128)}, f32[1,96,640]{2,1,0:T(8,128)}) fusion(f32[96,640]{1,0:T(8,128)} %get-tuple-element.6, f32[1,96,640]{2,1,0:T(8,128)} %param.15, f32[1,96,640]{2,1,0:T(8,128)} %param.14, f32[1,96,640]{2,1,0:T(8,128)} %param.13), kind=kLoop, calls=%fused_computation.6 | loop fusion | flops 921600 | bytes 1720320 | tf_op jit(solution)/shard_map/broadcast_in_dim | solution.py:625
  157.4 0.0 copy-done
  157.4 0.8 copy.15
  (1 shorter events, 0.0 us)
Async XLA Ops:
  155.0 2.4 %copy-start = (bf16[96,2560]{1,0:T(8,128)(2,1)S(1)}, bf16[96,2560]{1,0:T(8,128)(2,1)}, u32[]{:S(2)}) copy-start(bf16[96,2560]{1,0:T(8,128)(2,1)} %get-tuple-element.7) | copy-start | bytes 1474564
